TPU v7x, 128 devices: a whole 4x4x4 slice. The times are simulated.
128 devices in a mesh: gx: 8 (over y_lo, x), gy: 16 (over y_hi, z, core).
Axes of the slice: x: 4, y: 4 (y_hi: 2, y_lo: 2; y = y_hi * 2 + y_lo), z: 4, core: 2. Of those that a mesh axis runs over, the one named last changes fastest.
Arguments:
- input_beam: float32 [2, 4096, 4096], P(None, ('gx', 'gy')), may hold values from -6 to 6
- offsets: int32 [2], replicated, may hold values from 0 to 4096
- distances: float32 [2], replicated, may hold values from 20 to 80
- screens: int32 [1, 8192, 8192], P(None, ('gx', 'gy')), may hold values from -127 to 127
- screen_scales: float32 [1, 64, 64], replicated, may hold values from 0.005 to 0.05
- last_screen: int32 [4096, 4096], P(('gx', 'gy')), may hold values from -127 to 127
- last_scales: float32 [32, 32], replicated, may hold values from 0.005 to 0.05
Outputs:
- output_beam: float32 [2, 4096, 4096], P(None, ('gx', 'gy'))
All inputs are finite; a program needn't handle non-finite values.
Results may differ from a plain program's by a relative error of at most 0.0001.
Values sent between devices are 32-bit elements; how exact they have to be, the bound alone decides.
No kernel may reach another device: no remote copies, remote signals or barrier semaphores. Data moves between devices by JAX's collectives and lax.ppermute only.
A program may use at most 128 MiB of HBM per device.

v0:
```python
import math

import jax
import jax.numpy as jnp
from jax import lax
from jax.sharding import PartitionSpec as P


def contract(pattern, lhs_array, rhs_array):
    return jnp.einsum(
        pattern,
        lhs_array,
        rhs_array,
        precision=lax.Precision.HIGHEST,
        preferred_element_type=jnp.float32,
    )


def angle_table(length, row_count, col_count, orient):
    row_ids = jnp.arange(row_count, dtype=jnp.int32)
    col_ids = jnp.arange(col_count, dtype=jnp.int32)
    product = row_ids[:, None] * col_ids[None, :] % length
    angles = product.astype(jnp.float32) * (2.0 * math.pi / length)
    return (jnp.cos(angles), orient * jnp.sin(angles))


def transform_last(planes, orient):
    shape_all = planes.shape
    length = shape_all[-1]
    inner_size = 128
    outer_size = length // inner_size
    grouped = planes.reshape((2, -1, outer_size, inner_size))
    real_part = grouped[0]
    imag_part = grouped[1]
    cos_outer, sin_outer = angle_table(outer_size, outer_size, outer_size, orient)
    first_real = contract("bpq,pk->bkq", real_part, cos_outer) - contract(
        "bpq,pk->bkq", imag_part, sin_outer
    )
    first_imag = contract("bpq,pk->bkq", real_part, sin_outer) + contract(
        "bpq,pk->bkq", imag_part, cos_outer
    )
    twiddle_cos, twiddle_sin = angle_table(length, outer_size, inner_size, orient)
    second_real = first_real * twiddle_cos - first_imag * twiddle_sin
    second_imag = first_real * twiddle_sin + first_imag * twiddle_cos
    cos_inner, sin_inner = angle_table(inner_size, inner_size, inner_size, orient)
    out_real = contract("bkq,qm->bmk", second_real, cos_inner) - contract(
        "bkq,qm->bmk", second_imag, sin_inner
    )
    out_imag = contract("bkq,qm->bmk", second_real, sin_inner) + contract(
        "bkq,qm->bmk", second_imag, cos_inner
    )
    return jnp.stack([out_real, out_imag]).reshape(shape_all)


def move_window(blocks):
    return lax.all_to_all(blocks, ("gx", "gy"), split_axis=1, concat_axis=1, tiled=True)


def move_grid(blocks):
    return lax.all_to_all(blocks, ("gx", "gy"), split_axis=1, concat_axis=1, tiled=True)


def to_columns(planes, mover, devices_total, col_count):
    row_count = planes.shape[1]
    blocks = planes.reshape((2, row_count, devices_total, col_count)).transpose((0, 2, 3, 1))
    arrived = mover(blocks.reshape((2, devices_total, col_count * row_count)))
    arrived = arrived.reshape((2, devices_total, col_count, row_count)).transpose((0, 2, 1, 3))
    return arrived.reshape((2, col_count, devices_total * row_count))


def to_rows(planes, mover, devices_total):
    col_count = planes.shape[1]
    row_count = planes.shape[2] // devices_total
    blocks = planes.reshape((2, col_count, devices_total, row_count)).transpose((0, 2, 1, 3))
    arrived = mover(blocks.reshape((2, devices_total, col_count * row_count)))
    arrived = arrived.reshape((2, devices_total, col_count, row_count)).transpose((0, 3, 1, 2))
    return arrived.reshape((2, row_count, devices_total * col_count))


def block_scales(scales, first_row, row_count):
    block_total = scales.shape[0]
    block_ids = (first_row + jnp.arange(row_count, dtype=jnp.int32)) // 128
    onehot = (block_ids[:, None] == jnp.arange(block_total, dtype=jnp.int32)[None, :]).astype(
        jnp.float32
    )
    picked = jnp.dot(
        onehot, scales, precision=lax.Precision.HIGHEST, preferred_element_type=jnp.float32
    )
    return jnp.broadcast_to(picked[:, :, None], (row_count, block_total, 128)).reshape(
        (row_count, block_total * 128)
    )


def rotate_planes(planes, phases):
    cosine = jnp.cos(phases)
    sine = jnp.sin(phases)
    return jnp.stack([planes[0] * cosine - planes[1] * sine, planes[0] * sine + planes[1] * cosine])


def signed_index(indices, length):
    return jnp.where(indices < length // 2, indices, indices - length)


def body(input_beam, offsets, distances, screens, screen_scales, last_screen, last_scales):
    devices_total = lax.axis_size(("gx", "gy"))
    position = lax.axis_index(("gx", "gy"))
    grid_size = screens.shape[2]
    window_size = input_beam.shape[2]
    beam_rows = input_beam.shape[1]
    grid_rows = screens.shape[1]
    col_count = grid_size // devices_total
    step_total = distances.shape[0]
    zero_index = jnp.zeros((), jnp.int32)
    phase_coef = (2.0 * math.pi / grid_size) ** 2
    col_ids = signed_index(position * col_count + jnp.arange(col_count, dtype=jnp.int32), grid_size)
    row_ids = signed_index(jnp.arange(grid_size, dtype=jnp.int32), grid_size)
    squared = (col_ids[:, None] * col_ids[:, None] + row_ids[None, :] * row_ids[None, :]).astype(
        jnp.float32
    )
    crop_start = (grid_size - window_size) // 2
    scaling = 1.0 / grid_size
    beam_field = input_beam
    for layer_index in range(step_total):
        if layer_index == 0:
            padded = jnp.zeros((2, beam_rows, grid_size), jnp.float32)
            padded = lax.dynamic_update_slice(
                padded, input_beam, (zero_index, zero_index, offsets[1])
            )
            columns = to_columns(
                transform_last(padded, -1.0), move_window, devices_total, col_count
            )
            spectral = jnp.zeros((2, col_count, grid_size), jnp.float32)
            spectral = lax.dynamic_update_slice(
                spectral, columns, (zero_index, zero_index, offsets[0])
            )
        else:
            spectral = to_columns(
                transform_last(beam_field, -1.0), move_grid, devices_total, col_count
            )
        spectrum = transform_last(spectral, -1.0)
        phases = squared * (distances[layer_index] * phase_coef)
        spectrum = rotate_planes(spectrum, -phases)
        mixed = transform_last(spectrum, 1.0) * scaling
        if layer_index < step_total - 1:
            row_planes = to_rows(mixed, move_grid, devices_total)
            beam_field = transform_last(row_planes, 1.0) * scaling
            screen_phase = block_scales(
                screen_scales[layer_index], position * grid_rows, grid_rows
            ) * screens[layer_index].astype(jnp.float32)
            beam_field = rotate_planes(beam_field, screen_phase)
        else:
            cropped = mixed[:, :, crop_start : crop_start + window_size]
            row_planes = to_rows(cropped, move_window, devices_total)
            beam_field = transform_last(row_planes, 1.0) * scaling
            beam_field = beam_field[:, :, crop_start : crop_start + window_size]
            out_rows = beam_field.shape[1]
            last_phase = block_scales(
                last_scales, position * out_rows, out_rows
            ) * last_screen.astype(jnp.float32)
            beam_field = rotate_planes(beam_field, last_phase)
    return beam_field


def solution(mesh):
    return jax.shard_map(
        body,
        mesh=mesh,
        in_specs=(
            P(None, ("gx", "gy"), None),
            P(),
            P(),
            P(None, ("gx", "gy"), None),
            P(),
            P(("gx", "gy"), None),
            P(),
        ),
        out_specs=P(None, ("gx", "gy"), None),
        check_vma=False,
    )
```

profile of v0, /device:TPU:1, one launch (start us, length us, event | category | flops | bytes accessed | tf_op | source)
XLA Modules:
  0.0 649.6 jit_solution(745161635449595609)
XLA Ops:
  21.5 11.9 %all-to-all-start = ((f32[2,128,2048]{2,0,1:T(2,128)}), f32[2,128,2048]{2,0,1:T(2,128)}, u32[]{:S(2)}, u32[]{:S(2)}) async-start(f32[2,128,2048]{2,0,1:T(2,128)} %copy.52), calls=%async_computation | async-start | bytes 4194304 | tf_op jit(solution)/shard_map/all_to_all | solution.py:56
  36.7 26.8 %all-to-all-done = f32[2,128,2048]{2,0,1:T(2,128)} async-done(((f32[2,128,2048]{2,0,1:T(2,128)}), f32[2,128,2048]{2,0,1:T(2,128)}, u32[]{:S(2)}, u32[]{:S(2)}) %all-to-all-start) | async-done | bytes 2097184 | tf_op jit(solution)/shard_map/all_to_all | solution.py:56
  76.1 11.2 %dynamic_update_slice.7 = f32[2,64,8192]{2,1,0:T(8,128)} dynamic-update-slice(f32[2,64,8192]{2,1,0:T(8,128)} %broadcast_in_dim.8, f32[2,64,4096]{2,1,0:T(8,128)S(1)} %copy.55, s32[]{:T(128)} %constant.149.clone.1, s32[]{:T(128)} %constant.149.clone.1, s32[]{:T(128)S(6)} %select_n.300) | dynamic-update-slice | bytes 4194308 | tf_op jit(solution)/shard_map/dynamic_update_slice | solution.py:133
  113.0 6.3 add_bitcast_fusion.5
  123.1 4.6 squeeze.87
  127.7 11.8 %fusion.194 = f32[64,64,128]{2,0,1:T(8,128)S(1)} fusion(f32[64,64,128]{2,1,0:T(8,128)} %squeeze.87, f32[64,64,128]{2,1,0:T(8,128)S(1)} %squeeze.86, f32[]{:T(128)} %bitcast.20, s32[64,128]{1,0:T(8,128)S(1)} %fusion.151, s32[64]{0:T(128)S(1)} %get-tuple-element.28), kind=kOutput, calls=%fused_computation.258 | convolution fusion | flops 406380544 | bytes 6324484 | tf_op jit(solution)/shard_map/bpq,pk->bkq/dot_general | solution.py:10
  139.6 9.6 %fusion.163 = f32[64,64,128]{2,0,1:T(8,128)S(1)} fusion(f32[64,64,128]{2,1,0:T(8,128)S(1)} %copy-done.3, f32[64,64,128]{2,1,0:T(8,128)S(1)} %squeeze.86, f32[]{:T(128)} %bitcast.20, s32[64,128]{1,0:T(8,128)S(1)} %fusion.151, s32[64]{0:T(128)S(1)} %get-tuple-element.28), kind=kOutput, calls=%fused_computation.227 | convolution fusion | flops 406380544 | bytes 6324484 | tf_op jit(solution)/shard_map/bpq,pk->bkq/dot_general | solution.py:10
  149.2 9.8 %convolution_subtract_fusion.4 = f32[64,64,128]{2,0,1:T(8,128)S(1)} fusion(f32[64,64,128]{2,0,1:T(8,128)S(1)} %fusion.194, f32[64,64,128]{2,1,0:T(8,128)S(1)} %copy-done.3, f32[64,64,128]{2,1,0:T(8,128)S(1)} %squeeze.86, f32[]{:T(128)} %bitcast.20, s32[64,128]{1,0:T(8,128)S(1)} %fusion.151, s32[64]{0:T(128)S(1)} %get-tuple-element.28), kind=kOutput, calls=%fused_computation.112 | convolution fusion | flops 406904832 | bytes 8421636 | tf_op jit(solution)/shard_map/bpq,pk->bkq/dot_general | solution.py:10
  159.1 10.0 %convolution_add_fusion.4 = f32[64,64,128]{2,0,1:T(8,128)S(1)} fusion(f32[64,64,128]{2,0,1:T(8,128)S(1)} %fusion.163, f32[64,64,128]{2,1,0:T(8,128)S(1)} %copy-done.3, f32[64,64,128]{2,1,0:T(8,128)S(1)} %squeeze.86, f32[]{:T(128)} %bitcast.20, s32[64,128]{1,0:T(8,128)S(1)} %fusion.151, s32[64]{0:T(128)S(1)} %get-tuple-element.28), kind=kOutput, calls=%fused_computation.111 | convolution fusion | flops 406904832 | bytes 8421636 | tf_op jit(solution)/shard_map/bpq,pk->bkq/dot_general | solution.py:10
  180.8 7.3 %copy.58 = f32[2,128,4096]{2,0,1:T(2,128)} copy(f32[2,128,4096]{1,2,0:T(8,128)} %bitcast.444) | data formatting | bytes 8388608 | tf_op jit(solution)/shard_map/reshape | solution.py:75
  188.1 5.4 all-to-all-start.1
  195.6 50.4 %all-to-all-done.1 = f32[2,128,4096]{2,0,1:T(2,128)} async-done(((f32[2,128,4096]{2,0,1:T(2,128)}), f32[2,128,4096]{2,0,1:T(2,128)}, u32[]{:S(2)}, u32[]{:S(2)}) %all-to-all-start.1) | async-done | bytes 4194336 | tf_op jit(solution)/shard_map/all_to_all | solution.py:60
  246.0 7.3 %copy.59 = f32[2,128,4096]{1,2,0:T(8,128)} copy(f32[2,128,4096]{2,0,1:T(2,128)} %all-to-all-done.1) | data formatting | bytes 8388608 | tf_op jit(solution)/shard_map/all_to_all | solution.py:60
  274.2 4.8 squeeze.89
  298.6 4.8 stack.84
  303.4 5.6 add_bitcast_fusion.3
  312.9 4.9 stack.85
  322.1 9.2 %fusion.1 = (f32[64,64,128]{2,1,0:T(8,128)S(1)}, f32[64,64,128]{2,1,0:T(8,128)S(1)}) fusion(f32[8,8,64,128]{3,2,1,0:T(8,128)S(1)} %copy.87, f32[8,8,64,128]{3,2,1,0:T(8,128)S(1)} %copy.85, f32[8,8,64,128]{3,2,1,0:T(8,128)S(1)} %copy-done.14, f32[64,64]{1,0:T(8,128)S(1)} %fusion.152), kind=kLoop, calls=%fused_computation.6 | loop fusion | flops 3670016 | bytes 10502144 | tf_op jit(solution)/shard_map/add | solution.py:97
  353.6 7.3 %copy.65 = f32[2,128,4096]{2,0,1:T(2,128)} copy(f32[2,128,4096]{1,2,0:T(8,128)} %bitcast.445) | data formatting | bytes 8388608 | tf_op jit(solution)/shard_map/reshape | solution.py:66
  360.9 8.1 %all-to-all-start.2 = ((f32[2,128,4096]{2,0,1:T(2,128)}), f32[2,128,4096]{2,0,1:T(2,128)}, u32[]{:S(2)}, u32[]{:S(2)}) async-start(f32[2,128,4096]{2,0,1:T(2,128)} %copy.65), calls=%async_computation.2 | async-start | bytes 8388608 | tf_op jit(solution)/shard_map/all_to_all | solution.py:60
  369.7 51.7 %all-to-all-done.2 = f32[2,128,4096]{2,0,1:T(2,128)} async-done(((f32[2,128,4096]{2,0,1:T(2,128)}), f32[2,128,4096]{2,0,1:T(2,128)}, u32[]{:S(2)}, u32[]{:S(2)}) %all-to-all-start.2) | async-done | bytes 4194336 | tf_op jit(solution)/shard_map/all_to_all | solution.py:60
  421.4 7.3 %copy.66 = f32[2,128,4096]{1,2,0:T(8,128)} copy(f32[2,128,4096]{2,0,1:T(2,128)} %all-to-all-done.2) | data formatting | bytes 8388608 | tf_op jit(solution)/shard_map/all_to_all | solution.py:60
  473.3 6.3 add_bitcast_fusion.1
  488.1 11.6 %fusion.182 = f32[64,64,128]{2,0,1:T(8,128)S(1)} fusion(f32[64,64,128]{2,1,0:T(8,128)} %squeeze.96, f32[64,64,128]{2,1,0:T(8,128)S(1)} %squeeze.95, f32[]{:T(128)} %bitcast.54, s32[64,128]{1,0:T(8,128)S(1)} %fusion.151, s32[64]{0:T(128)S(1)} %get-tuple-element.28), kind=kOutput, calls=%fused_computation.246 | convolution fusion | flops 406380544 | bytes 6324484 | tf_op jit(solution)/shard_map/bpq,pk->bkq/dot_general | solution.py:10
  499.7 9.6 %fusion.157 = f32[64,64,128]{2,0,1:T(8,128)S(1)} fusion(f32[64,64,128]{2,1,0:T(8,128)S(1)} %copy-done.2, f32[64,64,128]{2,1,0:T(8,128)S(1)} %squeeze.95, f32[]{:T(128)} %bitcast.54, s32[64,128]{1,0:T(8,128)S(1)} %fusion.151, s32[64]{0:T(128)S(1)} %get-tuple-element.28), kind=kOutput, calls=%fused_computation.221 | convolution fusion | flops 406380544 | bytes 6324484 | tf_op jit(solution)/shard_map/bpq,pk->bkq/dot_general | solution.py:10
  509.3 9.9 %convolution_subtract_fusion = f32[64,64,128]{2,0,1:T(8,128)S(1)} fusion(f32[64,64,128]{2,0,1:T(8,128)S(1)} %fusion.182, f32[64,64,128]{2,1,0:T(8,128)S(1)} %copy-done.2, f32[64,64,128]{2,1,0:T(8,128)S(1)} %squeeze.95, f32[]{:T(128)} %bitcast.54, s32[64,128]{1,0:T(8,128)S(1)} %fusion.151, s32[64]{0:T(128)S(1)} %get-tuple-element.28), kind=kOutput, calls=%fused_computation.104 | convolution fusion | flops 406904832 | bytes 8421636 | tf_op jit(solution)/shard_map/bpq,pk->bkq/dot_general | solution.py:10
  519.2 10.2 %convolution_add_fusion = f32[64,64,128]{2,0,1:T(8,128)S(1)} fusion(f32[64,64,128]{2,0,1:T(8,128)S(1)} %fusion.157, f32[64,64,128]{2,1,0:T(8,128)S(1)} %copy-done.2, f32[64,64,128]{2,1,0:T(8,128)S(1)} %squeeze.95, f32[]{:T(128)} %bitcast.54, s32[64,128]{1,0:T(8,128)S(1)} %fusion.151, s32[64]{0:T(128)S(1)} %get-tuple-element.28), kind=kOutput, calls=%fused_computation.103 | convolution fusion | flops 406904832 | bytes 8421636 | tf_op jit(solution)/shard_map/bpq,pk->bkq/dot_general | solution.py:10
  540.1 4.9 stack.90
  545.0 5.7 add_bitcast_fusion
  554.5 4.9 stack.91
  573.0 8.0 %all-to-all-start.3 = ((f32[2,128,2048]{2,0,1:T(2,128)}), f32[2,128,2048]{2,0,1:T(2,128)S(1)}, u32[]{:S(2)}, u32[]{:S(2)}) async-start(f32[2,128,2048]{2,0,1:T(2,128)} %copy.75), calls=%async_computation.3 | async-start | bytes 4194304 | tf_op jit(solution)/shard_map/all_to_all | solution.py:56
  581.2 30.1 %all-to-all-done.3 = f32[2,128,2048]{2,0,1:T(2,128)S(1)} async-done(((f32[2,128,2048]{2,0,1:T(2,128)}), f32[2,128,2048]{2,0,1:T(2,128)S(1)}, u32[]{:S(2)}, u32[]{:S(2)}) %all-to-all-start.3) | async-done | bytes 2097184 | tf_op jit(solution)/shard_map/all_to_all | solution.py:56
  (171 shorter events, 265.7 us)
Async XLA Ops:
  0.0 195.4 %copy-start = (f32[1,64,64]{2,1,0:T(8,128)S(1)}, f32[1,64,64]{2,1,0:T(8,128)}, u32[]{:S(2)}) copy-start(f32[1,64,64]{2,1,0:T(8,128)} %param.11) | copy-start | bytes 49156
  0.0 3.6 copy-start.20
  21.5 13.9 %copy-start.22 = (f32[2]{0:T(128)S(1)}, f32[2]{0:T(128)}, u32[]{:S(2)}) copy-start(f32[2]{0:T(128)} %param.9) | copy-start | bytes 28
  21.5 42.0 %all-to-all-start = ((f32[2,128,2048]{2,0,1:T(2,128)}), f32[2,128,2048]{2,0,1:T(2,128)}, u32[]{:S(2)}, u32[]{:S(2)}) async-start(f32[2,128,2048]{2,0,1:T(2,128)} %copy.52), calls=%async_computation | async-start | bytes 4194304 | tf_op jit(solution)/shard_map/all_to_all | solution.py:56
  96.9 8.0 %copy-start.8 = (f32[64,64,128]{2,0,1:T(8,128)}, f32[64,64,128]{2,0,1:T(8,128)S(1)}, u32[]{:S(2)}) copy-start(f32[64,64,128]{2,0,1:T(8,128)S(1)} %convolution_subtract_fusion.5) | copy-start | bytes 6291460
  99.1 5.8 copy-start.10
  127.7 11.8 %copy-start.3 = (f32[64,64,128]{2,1,0:T(8,128)S(1)}, f32[64,64,128]{2,1,0:T(8,128)}, u32[]{:S(2)}) copy-start(f32[64,64,128]{2,1,0:T(8,128)} %squeeze.87) | copy-start | bytes 6291460
  188.1 5.4 copy-start.19
  188.1 57.9 %all-to-all-start.1 = ((f32[2,128,4096]{2,0,1:T(2,128)}), f32[2,128,4096]{2,0,1:T(2,128)}, u32[]{:S(2)}, u32[]{:S(2)}) async-start(f32[2,128,4096]{2,0,1:T(2,128)} %copy.58), calls=%async_computation.1 | async-start | bytes 8388608 | tf_op jit(solution)/shard_map/all_to_all | solution.py:60
  279.0 4.4 copy-start.12
  279.0 4.4 copy-start.15
  285.6 5.7 copy-start.11
  312.9 4.9 copy-start.17
  320.5 1.6 copy-start.14
  360.9 60.5 %all-to-all-start.2 = ((f32[2,128,4096]{2,0,1:T(2,128)}), f32[2,128,4096]{2,0,1:T(2,128)}, u32[]{:S(2)}, u32[]{:S(2)}) async-start(f32[2,128,4096]{2,0,1:T(2,128)} %copy.65), calls=%async_computation.2 | async-start | bytes 8388608 | tf_op jit(solution)/shard_map/all_to_all | solution.py:60
  453.0 4.0 copy-start.16
  457.0 7.8 %copy-start.7 = (f32[64,64,128]{2,0,1:T(8,128)}, f32[64,64,128]{2,0,1:T(8,128)S(1)}, u32[]{:S(2)}) copy-start(f32[64,64,128]{2,0,1:T(8,128)S(1)} %convolution_subtract_fusion.1) | copy-start | bytes 6291460
  459.2 5.6 copy-start.9
  488.0 11.6 %copy-start.2 = (f32[64,64,128]{2,1,0:T(8,128)S(1)}, f32[64,64,128]{2,1,0:T(8,128)}, u32[]{:S(2)}) copy-start(f32[64,64,128]{2,1,0:T(8,128)} %squeeze.96) | copy-start | bytes 6291460
  519.2 15.8 %copy-start.4 = (f32[64,64,128]{2,0,1:T(8,128)}, f32[64,64,128]{2,0,1:T(8,128)S(1)}, u32[]{:S(2)}) copy-start(f32[64,64,128]{2,0,1:T(8,128)S(1)} %convolution_subtract_fusion) | copy-start | bytes 6291460
  529.4 5.7 copy-start.6
  540.1 4.9 copy-start.5
  554.5 4.9 copy-start.13
  573.0 8.0 %copy-start.23 = (f32[32,32]{1,0:T(8,128)S(1)}, f32[32,32]{1,0:T(8,128)}, u32[]{:S(2)}) copy-start(f32[32,32]{1,0:T(8,128)} %param.13) | copy-start | bytes 12292
  573.0 38.3 %all-to-all-start.3 = ((f32[2,128,2048]{2,0,1:T(2,128)}), f32[2,128,2048]{2,0,1:T(2,128)S(1)}, u32[]{:S(2)}, u32[]{:S(2)}) async-start(f32[2,128,2048]{2,0,1:T(2,128)} %copy.75), calls=%async_computation.3 | async-start | bytes 4194304 | tf_op jit(solution)/shard_map/all_to_all | solution.py:56
  624.7 2.5 copy-start.18
  644.3 1.7 copy-start.21
  645.9 3.3 copy-start.1
where the time goes:
time: 661 us; the launch traced here: 650 us
  matrix products  227 us (34%)
  local copies, waits for them, and re-layouts  202 us (31%)
  waiting for transfers between devices  159 us (24%)
  starting transfers between devices  33.4 us (5%)
  other arithmetic  22.3 us (3%)
    dot_general x64, matrix products, contract(): jnp.einsum(pattern, lhs_array, rhs_array, precision=lax.Precision.HIGHEST...  226 us
    all_to_all x2, waiting for transfers between devices, move_grid(): lax.all_to_all(blocks, ('gx', 'gy'), split_axis=1, concat_axis=1, tiled=T...  102 us
    all_to_all x2, waiting for transfers between devices, move_window(): lax.all_to_all(blocks, ('gx', 'gy'), split_axis=1, concat_axis=1, tiled=T...  57 us
    another operation x6, local copies, waits for them, and re-layouts, transform_last(): return jnp.stack([out_real, out_imag]).reshape(shape_all)  23.6 us
    all_to_all x2, starting transfers between devices, move_window(): lax.all_to_all(blocks, ('gx', 'gy'), split_axis=1, concat_axis=1, tiled=T...  19.9 us
    slice x6, local copies, waits for them, and re-layouts, transform_last(): imag_part = grouped[1]  18.1 us
    add x5, local copies, waits for them, and re-layouts, transform_last(): contract('bkq,qm->bmk', second_real, sin_inner)  17.1 us
    all_to_all x2, local copies, waits for them, and re-layouts, move_grid(): lax.all_to_all(blocks, ('gx', 'gy'), split_axis=1, concat_axis=1, tiled=T...  14.5 us
  transfers between devices with their start and end apart: 4, of which 4 were waited for; matrix products, arithmetic and copies ran while one was open for 0% of the time, Pallas kernels for 0%

commit v1 on v0

v1 whole, which is shorter than its diff:
```python
import math

import jax
import jax.numpy as jnp
import numpy as np
from jax import lax
from jax.experimental import pallas as pl
from jax.experimental.pallas import tpu as pltpu
from jax.sharding import PartitionSpec as P

N = 8192
LANES = 128
AXES = ("gx", "gy")
ROOT_HALF = math.sqrt(0.5)
F32 = jnp.float32
BF16 = jnp.bfloat16


def constant_tables():
    k1 = np.arange(8)[:, None] + 8 * np.arange(8)[None, :]
    angle = -2.0 * np.pi * (k1[:, :, None] * np.arange(LANES)[None, None, :]) / N
    twiddle = np.stack([np.cos(angle), np.sin(angle)]).astype(np.float32)
    lane = np.arange(LANES)
    angle = -2.0 * np.pi * ((lane[:, None] * lane[None, :]) % LANES) / LANES
    cosine, sine = np.cos(angle), np.sin(angle)
    full = np.block([[cosine, sine], [-sine, cosine]]).astype(np.float32)
    high = full.astype(jnp.bfloat16)
    low = (full - high.astype(np.float32)).astype(jnp.bfloat16)
    return twiddle, np.concatenate([high, high, low])


def c_add(x, y):
    if x is None:
        return y
    if y is None:
        return x
    return (x[0] + y[0], x[1] + y[1])


def c_sub(x, y):
    if y is None:
        return x
    if x is None:
        return (-y[0], -y[1])
    return (x[0] - y[0], x[1] - y[1])


def c_mul(x, y):
    return (x[0] * y[0] - x[1] * y[1], x[0] * y[1] + x[1] * y[0])


def c_mul_conj(x, y):
    return (x[0] * y[0] + x[1] * y[1], x[1] * y[0] - x[0] * y[1])


def turn(x, sign):
    if x is None:
        return None
    return (-x[1], x[0]) if sign > 0 else (x[1], -x[0])


def eighth(x, sign):
    if x is None:
        return None
    if sign > 0:
        return ((x[0] - x[1]) * ROOT_HALF, (x[1] + x[0]) * ROOT_HALF)
    return ((x[0] + x[1]) * ROOT_HALF, (x[1] - x[0]) * ROOT_HALF)


def radix4(x0, x1, x2, x3, sign):
    even_sum, even_diff = c_add(x0, x2), c_sub(x0, x2)
    odd_sum, odd_diff = c_add(x1, x3), turn(c_sub(x1, x3), sign)
    return [
        c_add(even_sum, odd_sum),
        c_add(even_diff, odd_diff),
        c_sub(even_sum, odd_sum),
        c_sub(even_diff, odd_diff),
    ]


def radix8(x, sign):
    even = radix4(x[0], x[2], x[4], x[6], sign)
    odd = radix4(x[1], x[3], x[5], x[7], sign)
    odd[1] = eighth(odd[1], sign)
    odd[2] = turn(odd[2], sign)
    odd[3] = turn(eighth(odd[3], sign), sign)
    return [c_add(even[i], odd[i]) for i in range(4)] + [
        c_sub(even[i], odd[i]) for i in range(4)
    ]


def unit_root(x, index, sign):
    index = index % 64
    if index == 0:
        return x
    if index == 8:
        return eighth(x, sign)
    if index == 16:
        return turn(x, sign)
    angle = 2.0 * math.pi * index / 64
    return c_mul(x, (math.cos(angle), sign * math.sin(angle)))


def sincos(angle):
    turns = jnp.floor(angle * (2.0 / math.pi) + 0.5)
    rest = angle - turns * 1.5703125
    rest = rest - turns * 4.837512969970703125e-4
    rest = rest - turns * 7.54978995489188216e-8
    square = rest * rest
    sine = rest + rest * square * (
        -1.6666654611e-1 + square * (8.3321608736e-3 - square * 1.9515295891e-4)
    )
    cosine = (
        1.0
        - 0.5 * square
        + square
        * square
        * (4.166664568298827e-2 + square * (-1.388731625493765e-3 + square * 2.443315711809948e-5))
    )
    quarter = turns.astype(jnp.int32)
    swap = (quarter & 1) == 1
    sin_part = jnp.where(swap, cosine, sine)
    cos_part = jnp.where(swap, sine, cosine)
    sin_out = jnp.where((quarter & 2) == 2, -sin_part, sin_part)
    cos_out = jnp.where(((quarter + 1) & 2) == 2, -cos_part, cos_part)
    return cos_out, sin_out


def transfer_table(table, distance, offset):
    shape = (8, LANES)
    q_ids = lax.broadcasted_iota(jnp.int32, shape, 0)
    lane_ids = lax.broadcasted_iota(jnp.int32, shape, 1)
    coef = jnp.full(shape, distance, F32) * ((2.0 * math.pi / N) ** 2)
    coef1 = coef.astype(BF16).astype(F32)
    coef2 = (coef - coef1).astype(BF16).astype(F32)
    coef3 = (coef - coef1) - coef2
    for p in range(8):
        k = p + 8 * q_ids + 64 * lane_ids
        k = jnp.where(k < N // 2, k, k - N)
        squared = k * k
        upper = (squared & ~4095).astype(F32)
        lower = (squared & 4095).astype(F32)
        top = coef1 * upper
        turns = jnp.floor(top * (0.5 / math.pi) + 0.5)
        rest = (top - turns * 6.28125) - turns * 1.9350051879882812e-3
        rest = rest - turns * 3.0199159819567529e-7
        rest = rest + (coef2 * upper + (coef1 * lower + (coef3 * upper + coef2 * lower)))
        ramp = (k * offset) & (N - 1)
        ramp = jnp.where(ramp < N // 2, ramp, ramp - N).astype(F32) * (2.0 * math.pi / N)
        cosine, sine = sincos(rest + ramp)
        table[0, p] = cosine * (1.0 / N)
        table[1, p] = sine * (-1.0 / N)


def split_pair(first, second):
    both = jnp.concatenate([first, second], axis=0)
    high = both.astype(BF16)
    low = (both - high.astype(F32)).astype(BF16)
    return high, low


def store_split(lhs, row, values, lane):
    for half in range(4):
        high, low = split_pair(values[2 * half], values[2 * half + 1])
        rows = pl.ds(row + 16 * half, 16)
        lhs[rows, lane : lane + LANES] = high
        lhs[rows, 2 * LANES + lane : 3 * LANES + lane] = low


def product(lhs, weight):
    high, low = lhs[:, : 2 * LANES], lhs[:, 2 * LANES :]
    return jnp.dot(
        jnp.concatenate([high, low, high], axis=1), weight[...], preferred_element_type=F32
    )


def spectral_pass(field, table, twiddle, weight, lhs, result, batch):
    groups = batch // 8

    def per_p(p, carry):
        def row_of(values, part, q):
            return values[part, p, q : q + 1, :]

        for g in range(groups):
            rows = slice(8 * g, 8 * g + 8)
            x = radix8([(field[0, p, b, rows], field[1, p, b, rows]) for b in range(8)], -1)
            x = [c_mul(x[q], (row_of(twiddle, 0, q), row_of(twiddle, 1, q))) for q in range(8)]
            store_split(lhs, 64 * g, [v[0] for v in x], 0)
            store_split(lhs, 64 * g, [v[1] for v in x], LANES)
        result[...] = product(lhs, weight)
        for g in range(groups):
            x = []
            for q in range(8):
                rows = slice(64 * g + 8 * q, 64 * g + 8 * q + 8)
                value = (result[rows, :LANES], result[rows, LANES:])
                x.append(c_mul(value, (row_of(table, 0, q), row_of(table, 1, q))))
            store_split(lhs, 64 * g, [v[1] for v in x], 0)
            store_split(lhs, 64 * g, [v[0] for v in x], LANES)
        result[...] = product(lhs, weight)
        for g in range(groups):
            x = []
            for q in range(8):
                rows = slice(64 * g + 8 * q, 64 * g + 8 * q + 8)
                value = (result[rows, LANES:], result[rows, :LANES])
                x.append(c_mul_conj(value, (row_of(twiddle, 0, q), row_of(twiddle, 1, q))))
            x = radix8(x, 1)
            for b in range(8):
                rows = slice(8 * g, 8 * g + 8)
                field[0, p, b, rows] = x[b][0]
                field[1, p, b, rows] = x[b][1]
        return carry

    lax.fori_loop(0, 8, per_p, 0)


def enter(field, b, rows, x):
    x = radix8(x, -1)
    for p in range(8):
        value = unit_root(x[p], b * p, -1)
        field[0, p, b, rows] = value[0]
        field[1, p, b, rows] = value[1]


def leave(field, b, rows):
    x = [unit_root((field[0, p, b, rows], field[1, p, b, rows]), b * p, 1) for p in range(8)]
    return radix8(x, 1)


def low_half(shape):
    return lax.broadcasted_iota(jnp.int32, shape, len(shape) - 1) < LANES // 2


def swap_halves(even, odd, low):
    first = jnp.where(low, even, pltpu.roll(odd, LANES // 2, 1))
    second = jnp.where(low, pltpu.roll(even, LANES // 2, 1), odd)
    return first, second


def pack_screen_kernel(screen, packed):
    low = low_half((32, LANES))

    def per_tile(j, carry):
        tile = screen[0, :, pl.ds(pl.multiple_of(j * LANES, LANES), LANES)].astype(F32)
        even, odd = swap_halves(tile[:32], tile[32:], low)
        packed[2 * j] = even
        packed[2 * j + 1] = odd
        return carry

    lax.fori_loop(0, N // LANES, per_tile, 0, unroll=4)


def first_rows_kernel(offsets, distances, beam, twiddle, weight, moved, field, table, lhs, result):
    transfer_table(table, distances[0], offsets[1])
    low = low_half((8, LANES))

    def rows_of(g):
        return pl.ds(pl.multiple_of(g * 8, 8), 8)

    def first(g, carry):
        rows = rows_of(g)
        for b in range(8):
            x = []
            for a in range(8):
                n1 = 8 * a + b
                lanes = slice(n1 * LANES, (n1 + 1) * LANES)
                x.append((beam[0, rows, lanes], beam[1, rows, lanes]) if a < 4 else None)
            enter(field, b, rows, x)
        return carry

    lax.fori_loop(0, 4, first, 0)
    spectral_pass(field, table, twiddle, weight, lhs, result, 32)

    def last(g, carry):
        rows = rows_of(g)
        for b in range(8):
            x = leave(field, b, rows)
            for a in range(8):
                n1 = 8 * a + b
                even, odd = swap_halves(x[a][0], x[a][1], low)
                moved[2 * n1, rows] = even
                moved[2 * n1 + 1, rows] = odd
        return carry

    lax.fori_loop(0, 4, last, 0)


def columns_kernel(
    offsets, distances, scales, arrived, screen, twiddle, weight, moved,
    field, table, lhs, result, turned, phases,
):
    device = lax.axis_index(AXES)
    transfer_table(table, distances[0], offsets[0])
    lane = lax.broadcasted_iota(jnp.int32, (64, LANES), 1)

    def screens(s, carry):
        block = screen[pl.ds(pl.multiple_of(s * LANES, LANES), LANES), :].T
        upper, lower = block[:64], block[64:]
        upper32, lower32 = pltpu.roll(upper, 32, 1), pltpu.roll(lower, 32, 1)
        upper64, lower64 = pltpu.roll(upper, 64, 1), pltpu.roll(lower, 64, 1)
        upper96, lower96 = pltpu.roll(upper, 96, 1), pltpu.roll(lower, 96, 1)
        even = jnp.where(
            lane < 32, upper, jnp.where(lane < 64, lower32, jnp.where(lane < 96, upper32, lower64))
        )
        odd = jnp.where(
            lane < 32, upper64, jnp.where(lane < 64, lower96, jnp.where(lane < 96, upper96, lower))
        )
        phases[2 * s] = even * scales[0, 2 * s, device // 2]
        phases[2 * s + 1] = odd * scales[0, 2 * s + 1, device // 2]
        return carry

    lax.fori_loop(0, 32, screens, 0)

    def turn_in(n1, carry):
        turned[n1] = arrived[pl.ds(pl.multiple_of(n1 * LANES, LANES), LANES), :].T
        return carry

    lax.fori_loop(0, 32, turn_in, 0)

    def rows_of(g):
        start = pl.multiple_of(g * 8, 8)
        return pl.ds(start, 8), pl.ds(start + 64, 8)

    def first(g, carry):
        rows, rows_imag = rows_of(g)
        for b in range(8):
            x = [
                (turned[8 * a + b, rows], turned[8 * a + b, rows_imag]) if a < 4 else None
                for a in range(8)
            ]
            enter(field, b, rows, x)
        return carry

    lax.fori_loop(0, 8, first, 0)
    spectral_pass(field, table, twiddle, weight, lhs, result, 64)
    transfer_table(table, distances[1], jnp.int32(0))

    def middle(g, carry):
        rows, _ = rows_of(g)
        for b in range(8):
            x = leave(field, b, rows)
            x = [c_mul(x[a], sincos(phases[8 * a + b, rows])) for a in range(8)]
            enter(field, b, rows, x)
        return carry

    lax.fori_loop(0, 8, middle, 0)
    spectral_pass(field, table, twiddle, weight, lhs, result, 64)

    def last(g, carry):
        rows, rows_imag = rows_of(g)
        for b in range(8):
            x = leave(field, b, rows)
            for a in range(4):
                turned[8 * a + b, rows] = x[a + 2][0]
                turned[8 * a + b, rows_imag] = x[a + 2][1]
        return carry

    lax.fori_loop(0, 8, last, 0)

    def turn_out(n1, carry):
        moved[pl.ds(pl.multiple_of(n1 * LANES, LANES), LANES), :] = turned[n1].T
        return carry

    lax.fori_loop(0, 32, turn_out, 0)


def last_rows_kernel(
    distances, scales, arrived, screen, twiddle, weight, output, field, table, lhs, result
):
    device = lax.axis_index(AXES)
    transfer_table(table, distances[1], jnp.int32(0))
    low = low_half((8, LANES))

    def rows_of(g):
        return pl.ds(pl.multiple_of(g * 8, 8), 8)

    def first(g, carry):
        rows = rows_of(g)
        for b in range(8):
            x = []
            for a in range(8):
                n1 = 8 * a + b
                x.append(swap_halves(arrived[2 * n1, rows], arrived[2 * n1 + 1, rows], low))
            enter(field, b, rows, x)
        return carry

    lax.fori_loop(0, 4, first, 0)
    spectral_pass(field, table, twiddle, weight, lhs, result, 32)

    def last(g, carry):
        rows = rows_of(g)
        for b in range(8):
            x = leave(field, b, rows)
            for a in range(4):
                n1 = 8 * a + b
                lanes = slice(n1 * LANES, (n1 + 1) * LANES)
                phase = screen[rows, lanes].astype(F32) * scales[device // 4, n1]
                value = c_mul(x[a + 2], sincos(phase))
                output[0, rows, lanes] = value[0]
                output[1, rows, lanes] = value[1]
        return carry

    lax.fori_loop(0, 4, last, 0)


def call(kernel, kinds, shape, batch, extra, flops):
    space = {"s": pltpu.SMEM, "v": pltpu.VMEM}
    scratch = [
        pltpu.VMEM((2, 8, 8, batch, LANES), F32),
        pltpu.VMEM((2, 8, 8, LANES), F32),
        pltpu.VMEM((8 * batch, 4 * LANES), BF16),
        pltpu.VMEM((8 * batch, 2 * LANES), F32),
    ] if batch else []
    return pl.pallas_call(
        kernel,
        out_shape=jax.ShapeDtypeStruct(shape, F32),
        in_specs=[pl.BlockSpec(memory_space=space[kind]) for kind in kinds],
        out_specs=pl.BlockSpec(memory_space=pltpu.VMEM),
        scratch_shapes=scratch + extra,
        compiler_params=pltpu.CompilerParams(vmem_limit_bytes=48 << 20),
        cost_estimate=pl.CostEstimate(flops=flops, bytes_accessed=4 << 20, transcendentals=0),
    )


def exchange(blocks):
    return lax.all_to_all(blocks, AXES, split_axis=0, concat_axis=0, tiled=True)


def body(input_beam, offsets, distances, screens, screen_scales, last_screen, last_scales):
    twiddle, weight = (jnp.asarray(array) for array in constant_tables())
    blocks = (128, 32, LANES)
    packed = call(pack_screen_kernel, "v", blocks, 0, [], 1 << 20)(screens)
    screen_columns = exchange(packed).reshape((4096, LANES))
    moved = call(first_rows_kernel, "ssvvv", blocks, 32, [], 10**10)(
        offsets, distances, input_beam, twiddle, weight
    )
    arrived = exchange(moved).reshape((4096, LANES))
    extra = [pltpu.VMEM((32, LANES, LANES), F32), pltpu.VMEM((64, 64, LANES), F32)]
    moved = call(columns_kernel, "sssvvvv", (4096, LANES), 64, extra, 4 * 10**10)(
        offsets, distances, screen_scales, arrived, screen_columns, twiddle, weight
    )
    arrived = exchange(moved.reshape(blocks))
    return call(last_rows_kernel, "ssvvvv", (2, 32, 4096), 32, [], 10**10)(
        distances, last_scales, arrived, last_screen, twiddle, weight
    )


def solution(mesh):
    return jax.shard_map(
        body,
        mesh=mesh,
        in_specs=(
            P(None, AXES, None),
            P(),
            P(),
            P(None, AXES, None),
            P(),
            P(AXES, None),
            P(),
        ),
        out_specs=P(None, AXES, None),
        check_vma=False,
    )
```

time: 661 us -> 174 us (0.26); the launches traced: 650 us -> 173 us
  matrix products: 227 us -> 0 us
  local copies, waits for them, and re-layouts: 202 us -> 6 us
  waiting for transfers between devices: 159 us -> 26.8 us
  blocking collectives: 0 us -> 69.7 us
  Pallas kernels: 0 us -> 58.6 us
  other arithmetic: 22.3 us -> 0 us
  starting transfers between devices: 33.4 us -> 11.9 us
    dot_general x66 -> x0, matrix products: 227 us -> none  [the longest x64 226 us: contract(): jnp.einsum(pattern, lhs_array, rhs_array, precision=lax.Precision.HIGHEST...]
    all_to_all x4 -> x1, waiting for transfers between devices: 159 us -> 26.8 us  [exchange(): return lax.all_to_all(blocks, AXES, split_axis=0, concat_axis=0, tiled=True)]
    all_to_all x0 -> x2, blocking collectives: none -> 69.7 us  [exchange(): return lax.all_to_all(blocks, AXES, split_axis=0, concat_axis=0, tiled=True)]
    pallas_call x0 -> x4, Pallas kernels: none -> 58.6 us  [the longest x1 39 us: body(): call(columns_kernel, 'sssvvvv', (4096, LANES), 64, extra, 4 * 10 ** 10)]
    squeeze x10 -> x0, local copies, waits for them, and re-layouts: 33.1 us -> none  [the longest x2 9.25 us: rotate_planes(): planes[1] * sine]
    slice x12 -> x0, local copies, waits for them, and re-layouts: 31.5 us -> none  [the longest x6 18.1 us: transform_last(): imag_part = grouped[1]]
    another operation x6 -> x0, local copies, waits for them, and re-layouts: 23.6 us -> none  [transform_last(): return jnp.stack([out_real, out_imag]).reshape(shape_all)]
    reshape x5 -> x0, local copies, waits for them, and re-layouts: 22.3 us -> none  [the longest x2 9.78 us: to_rows(): arrived = mover(blocks.reshape((2, devices_total, col_count * row_count)))]
  transfers between devices with their start and end apart: 4 -> 1, of which waited for: 4 -> 1; matrix products, arithmetic and copies ran while one was open for 0% -> 0% of each run, Pallas kernels for 0% -> 1%
where the time goes in v1:
time: 174 us; the launch traced here: 173 us
  blocking collectives  69.7 us (40%)
  Pallas kernels  58.6 us (34%)
  waiting for transfers between devices  26.8 us (15%)
  starting transfers between devices  11.9 us (7%)
  local copies, waits for them, and re-layouts  6 us (3%)
    all_to_all x2, blocking collectives, exchange(): return lax.all_to_all(blocks, AXES, split_axis=0, concat_axis=0, tiled=True)  69.7 us
    pallas_call x1, Pallas kernels, body(): call(columns_kernel, 'sssvvvv', (4096, LANES), 64, extra, 4 * 10 ** 10)  39 us
    all_to_all x1, waiting for transfers between devices, exchange(): return lax.all_to_all(blocks, AXES, split_axis=0, concat_axis=0, tiled=True)  26.8 us
    all_to_all x1, starting transfers between devices, exchange(): return lax.all_to_all(blocks, AXES, split_axis=0, concat_axis=0, tiled=True)  11.9 us
    pallas_call x1, Pallas kernels, body(): call(last_rows_kernel, 'ssvvvv', (2, 32, 4096), 32, [], 10 ** 10)  9.41 us
    pallas_call x1, Pallas kernels, body(): call(first_rows_kernel, 'ssvvv', blocks, 32, [], 10 ** 10)  8.58 us
    unnamed x26, local copies, waits for them, and re-layouts  6 us
  transfers between devices with their start and end apart: 1, of which 1 were waited for; matrix products, arithmetic and copies ran while one was open for 0% of the time, Pallas kernels for 1%

profile of v1, /device:TPU:1, one launch (start us, length us, event | category | flops | bytes accessed | tf_op | source)
XLA Modules:
  0.0 173.2 jit_solution(14899931722218340814)
XLA Ops:
  0.0 0.0 copy-start.1
  0.0 1.2 copy-done.1
  1.2 0.0 copy-start.5
  1.2 0.7 copy-done.5
  1.9 0.0 copy-start.7
  1.9 0.7 copy-done.7
  2.5 1.0 copy-done.9
  3.5 0.8 copy-done.11
  4.4 8.6 %shard_map.91 = f32[128,32,128]{2,1,0:T(8,128)} custom-call(s32[2]{0:T(128)S(1)} %copy-done.5, f32[2]{0:T(128)S(1)} %copy-done.7, f32[2,32,4096]{2,1,0:T(8,128)S(1)} %copy-done.1, f32[2,8,8,128]{3,2,1,0:T(8,128)S(1)} %copy-done.11, bf16[768,256]{1,0:T(8,128)(2,1)S(1)} %copy-done.9), custom_call_target="tpu_custom_call" | custom-call | flops 10000000000 | bytes 4194304 | tf_op jit(solution)/shard_map/pallas_call | solution.py:433
  13.0 11.9 %all-to-all-start = ((f32[128,32,128]{2,1,0:T(8,128)}), f32[128,32,128]{2,1,0:T(8,128)}, u32[]{:S(2)}, u32[]{:S(2)}) async-start(f32[128,32,128]{2,1,0:T(8,128)} %shard_map.91), calls=%async_computation | async-start | bytes 4194304 | tf_op jit(solution)/shard_map/all_to_all | solution.py:425
  24.9 0.0 copy-start
  24.9 1.6 copy-done
  26.5 1.6 shard_map.92
  28.1 0.0 copy-start.3
  28.2 0.0 copy-start.6
  28.2 0.0 copy-start.8
  28.2 0.0 copy-start.10
  28.2 0.0 copy-start.12
  28.2 26.8 %all-to-all-done = f32[128,32,128]{2,1,0:T(8,128)} async-done(((f32[128,32,128]{2,1,0:T(8,128)}), f32[128,32,128]{2,1,0:T(8,128)}, u32[]{:S(2)}, u32[]{:S(2)}) %all-to-all-start) | async-done | bytes 2097184 | tf_op jit(solution)/shard_map/all_to_all | solution.py:425
  55.0 34.9 %all_to_all.15 = f32[128,32,128]{2,1,0:T(8,128)} all-to-all(f32[128,32,128]{2,1,0:T(8,128)S(1)} %shard_map.92), channel_id=1, replica_groups=mesh['gx'=8,'gy'=16] {'gx','gy'}, dimensions={0} | all-to-all | bytes 4194304 | tf_op jit(solution)/shard_map/all_to_all | solution.py:425
  89.9 0.0 copy-done.3
  89.9 0.0 copy-done.6
  89.9 0.0 copy-done.8
  89.9 0.0 copy-done.10
  89.9 0.0 copy-done.12
  89.9 39.0 %shard_map.93 = f32[4096,128]{1,0:T(8,128)S(1)} custom-call(s32[2]{0:T(128)S(1)} %copy-done.6, f32[2]{0:T(128)S(1)} %copy-done.8, f32[1,64,64]{2,1,0:T(8,128)S(1)} %copy-done.3, f32[4096,128]{1,0:T(8,128)} %bitcast.arrived, f32[4096,128]{1,0:T(8,128)} %bitcast.4, f32[2,8,8,128]{3,2,1,0:T(8,128)S(1)} %copy-done.12, bf16[768,256]{1,0:T(8,128)(2,1)S(1)} %copy-done.10), custom_call_target="tpu_custom_call" | custom-call | flops 40000000000 | bytes 4194304 | tf_op jit(solution)/shard_map/pallas_call | solution.py:438
  129.0 0.0 copy-start.2
  129.0 0.0 copy-start.4
  129.0 34.8 %all_to_all.16.arrived = f32[128,32,128]{2,1,0:T(8,128)S(1)} all-to-all(f32[128,32,128]{2,1,0:T(8,128)S(1)} %bitcast.3), channel_id=1, replica_groups=mesh['gx'=8,'gy'=16] {'gx','gy'}, dimensions={0} | all-to-all | bytes 4194304 | tf_op jit(solution)/shard_map/all_to_all | solution.py:425
  163.8 0.0 copy-done.2
  163.8 0.0 copy-done.4
  163.8 9.4 %shard_map.94 = f32[2,32,4096]{2,1,0:T(8,128)} custom-call(f32[2]{0:T(128)S(1)} %copy-done.8, f32[32,32]{1,0:T(8,128)S(1)} %copy-done.4, f32[128,32,128]{2,1,0:T(8,128)S(1)} %all_to_all.16.arrived, s32[32,4096]{1,0:T(8,128)S(1)} %copy-done.2, f32[2,8,8,128]{3,2,1,0:T(8,128)S(1)} %copy-done.12, bf16[768,256]{1,0:T(8,128)(2,1)S(1)} %copy-done.10), custom_call_target="tpu_custom_call" | custom-call | flops 10000000000 | bytes 4194304 | tf_op jit(solution)/shard_map/pallas_call | solution.py:442
  (2 shorter events, 0.0 us)
Async XLA Ops:
  0.0 1.2 copy-start.1
  1.2 0.7 copy-start.5
  1.9 0.7 copy-start.7
  2.5 1.0 copy-start.9
  3.5 0.8 copy-start.11
  13.0 42.1 %all-to-all-start = ((f32[128,32,128]{2,1,0:T(8,128)}), f32[128,32,128]{2,1,0:T(8,128)}, u32[]{:S(2)}, u32[]{:S(2)}) async-start(f32[128,32,128]{2,1,0:T(8,128)} %shard_map.91), calls=%async_computation | async-start | bytes 4194304 | tf_op jit(solution)/shard_map/all_to_all | solution.py:425
  24.9 1.6 copy-start
  28.1 61.8 %copy-start.3 = (f32[1,64,64]{2,1,0:T(8,128)S(1)}, f32[1,64,64]{2,1,0:T(8,128)}, u32[]{:S(2)}) copy-start(f32[1,64,64]{2,1,0:T(8,128)} %scales.2) | copy-start | bytes 49156
  28.2 61.8 %copy-start.6 = (s32[2]{0:T(128)S(1)}, s32[2]{0:T(128)}, u32[]{:S(2)}) copy-start(s32[2]{0:T(128)} %offsets.3) | copy-start | bytes 28
  28.2 61.8 %copy-start.8 = (f32[2]{0:T(128)S(1)}, f32[2]{0:T(128)}, u32[]{:S(2)}) copy-start(f32[2]{0:T(128)} %distances.5) | copy-start | bytes 28
  28.2 61.7 %copy-start.10 = (bf16[768,256]{1,0:T(8,128)(2,1)S(1)}, bf16[768,256]{1,0:T(8,128)(2,1)}, u32[]{:S(2)}) copy-start(bf16[768,256]{1,0:T(8,128)(2,1)} %constant.5.clone.weight) | copy-start | bytes 1179652
  28.2 61.7 %copy-start.12 = (f32[2,8,8,128]{3,2,1,0:T(8,128)S(1)}, f32[2,8,8,128]{3,2,1,0:T(8,128)}, u32[]{:S(2)}) copy-start(f32[2,8,8,128]{3,2,1,0:T(8,128)} %constant.4.clone.twiddle) | copy-start | bytes 196612
  129.0 34.8 %copy-start.2 = (s32[32,4096]{1,0:T(8,128)S(1)}, s32[32,4096]{1,0:T(8,128)}, u32[]{:S(2)}) copy-start(s32[32,4096]{1,0:T(8,128)} %screen.3) | copy-start | bytes 1572868
  129.0 34.8 %copy-start.4 = (f32[32,32]{1,0:T(8,128)S(1)}, f32[32,32]{1,0:T(8,128)}, u32[]{:S(2)}) copy-start(f32[32,32]{1,0:T(8,128)} %scales.3) | copy-start | bytes 12292

commit v2 on v1

--- a/solution.py
+++ b/solution.py
@@ -12,6 +12,14 @@
 LANES = 128
 AXES = ("gx", "gy")
 ROOT_HALF = math.sqrt(0.5)
+SINE = [
+    math.sqrt(2.0) * term
+    for term in (3.14159264013, -5.16771008351, 2.55007752321, -0.598291285620, 0.0776576603045)
+]
+COSINE = [
+    math.sqrt(2.0) * term
+    for term in (0.999999953248, -4.93479283062, 4.05841135286, -1.33187656808, 0.219689611098)
+]
 F32 = jnp.float32
 BF16 = jnp.bfloat16
 
@@ -124,6 +132,19 @@
     sin_out = jnp.where((quarter & 2) == 2, -sin_part, sin_part)
     cos_out = jnp.where(((quarter + 1) & 2) == 2, -cos_part, cos_part)
     return cos_out, sin_out
+
+
+def phasor(turns):
+    rest = turns - jnp.floor(turns + 0.5)
+    square = rest * rest
+    sine = rest * (
+        SINE[0]
+        + square * (SINE[1] + square * (SINE[2] + square * (SINE[3] + square * SINE[4])))
+    )
+    cosine = COSINE[0] + square * (
+        COSINE[1] + square * (COSINE[2] + square * (COSINE[3] + square * COSINE[4]))
+    )
+    return 1.0 - sine * sine, sine * cosine
 
 
 def transfer_table(table, distance, offset):
@@ -174,43 +195,88 @@
     )
 
 
-def spectral_pass(field, table, twiddle, weight, lhs, result, batch):
+def spectral_pass(field, table, twiddle, weight, left, result, batch):
     groups = batch // 8
-
-    def per_p(p, carry):
-        def row_of(values, part, q):
-            return values[part, p, q : q + 1, :]
-
-        for g in range(groups):
-            rows = slice(8 * g, 8 * g + 8)
+    width = 64 // batch
+    steps = 8 // width
+
+    def row_of(values, part, p, q):
+        return values[part, p, q : q + 1, :]
+
+    def places(step):
+        for j in range(width):
+            for g in range(groups):
+                yield step * width + j, slice(8 * g, 8 * g + 8), 64 * (groups * j + g)
+
+    def result_rows(row, q):
+        return slice(row + 8 * q, row + 8 * q + 8)
+
+    def forward(step, lhs):
+        for p, rows, row in places(step):
             x = radix8([(field[0, p, b, rows], field[1, p, b, rows]) for b in range(8)], -1)
-            x = [c_mul(x[q], (row_of(twiddle, 0, q), row_of(twiddle, 1, q))) for q in range(8)]
-            store_split(lhs, 64 * g, [v[0] for v in x], 0)
-            store_split(lhs, 64 * g, [v[1] for v in x], LANES)
-        result[...] = product(lhs, weight)
-        for g in range(groups):
+            x = [
+                c_mul(x[q], (row_of(twiddle, 0, p, q), row_of(twiddle, 1, p, q)))
+                for q in range(8)
+            ]
+            store_split(lhs, row, [v[0] for v in x], 0)
+            store_split(lhs, row, [v[1] for v in x], LANES)
+
+    def transfer(step, values, lhs):
+        for p, rows, row in places(step):
             x = []
             for q in range(8):
-                rows = slice(64 * g + 8 * q, 64 * g + 8 * q + 8)
-                value = (result[rows, :LANES], result[rows, LANES:])
-                x.append(c_mul(value, (row_of(table, 0, q), row_of(table, 1, q))))
-            store_split(lhs, 64 * g, [v[1] for v in x], 0)
-            store_split(lhs, 64 * g, [v[0] for v in x], LANES)
-        result[...] = product(lhs, weight)
-        for g in range(groups):
+                at = result_rows(row, q)
+                value = (values[at, :LANES], values[at, LANES:])
+                x.append(c_mul(value, (row_of(table, 0, p, q), row_of(table, 1, p, q))))
+            store_split(lhs, row, [v[1] for v in x], 0)
+            store_split(lhs, row, [v[0] for v in x], LANES)
+
+    def inverse(step, values):
+        for p, rows, row in places(step):
             x = []
             for q in range(8):
-                rows = slice(64 * g + 8 * q, 64 * g + 8 * q + 8)
-                value = (result[rows, LANES:], result[rows, :LANES])
-                x.append(c_mul_conj(value, (row_of(twiddle, 0, q), row_of(twiddle, 1, q))))
+                at = result_rows(row, q)
+                value = (values[at, LANES:], values[at, :LANES])
+                x.append(
+                    c_mul_conj(value, (row_of(twiddle, 0, p, q), row_of(twiddle, 1, p, q)))
+                )
             x = radix8(x, 1)
             for b in range(8):
-                rows = slice(8 * g, 8 * g + 8)
                 field[0, p, b, rows] = x[b][0]
                 field[1, p, b, rows] = x[b][1]
-        return carry
-
-    lax.fori_loop(0, 8, per_p, 0)
+
+    def multiply(lhs, values):
+        values[...] = product(lhs, weight)
+
+    forward_left, inverse_left = left[:2], left[2:]
+    forward_result, inverse_result = result[:2], result[2:]
+    forward(0, forward_left[0])
+    multiply(forward_left[0], forward_result[0])
+    forward(1, forward_left[1])
+    multiply(forward_left[1], forward_result[1])
+    transfer(0, forward_result[0], inverse_left[0])
+    multiply(inverse_left[0], inverse_result[0])
+    forward(2, forward_left[0])
+
+    def two_steps(i, carry):
+        step = 2 * i
+        multiply(forward_left[0], forward_result[0])
+        transfer(step - 1, forward_result[1], inverse_left[1])
+        multiply(inverse_left[1], inverse_result[1])
+        inverse(step - 2, inverse_result[0])
+        forward(step + 1, forward_left[1])
+        multiply(forward_left[1], forward_result[1])
+        transfer(step, forward_result[0], inverse_left[0])
+        multiply(inverse_left[0], inverse_result[0])
+        inverse(step - 1, inverse_result[1])
+        forward(jnp.minimum(step + 2, steps - 1), forward_left[0])
+        return carry
+
+    lax.fori_loop(1, steps // 2, two_steps, 0)
+    transfer(steps - 1, forward_result[1], inverse_left[1])
+    multiply(inverse_left[1], inverse_result[1])
+    inverse(steps - 2, inverse_result[0])
+    inverse(steps - 1, inverse_result[1])
 
 
 def enter(field, b, rows, x):
@@ -236,28 +302,64 @@
     return first, second
 
 
-def pack_screen_kernel(screen, packed):
+def eight_rows(g):
+    return pl.ds(pl.multiple_of(g * 8, 8), 8)
+
+
+def pack_screen(scales, screen, moved, device):
     low = low_half((32, LANES))
 
-    def per_tile(j, carry):
-        tile = screen[0, :, pl.ds(pl.multiple_of(j * LANES, LANES), LANES)].astype(F32)
-        even, odd = swap_halves(tile[:32], tile[32:], low)
-        packed[2 * j] = even
-        packed[2 * j + 1] = odd
-        return carry
-
-    lax.fori_loop(0, N // LANES, per_tile, 0, unroll=4)
-
-
-def first_rows_kernel(offsets, distances, beam, twiddle, weight, moved, field, table, lhs, result):
+    def per_pair(j, carry):
+        tiles = []
+        for half in range(2):
+            lanes = pl.ds(pl.multiple_of(j * (2 * LANES), 2 * LANES) + half * LANES, LANES)
+            scale = scales[0, device // 2, 2 * j + half] * (0.5 / math.pi)
+            tiles.append(screen[0, :, lanes].astype(F32) * scale)
+        block = jnp.concatenate(tiles, axis=0).T
+        for half in range(2):
+            part = block[64 * half : 64 * half + 64]
+            first, second = swap_halves(part[:32], part[32:], low)
+            moved[4 * j + half, 32:] = first
+            moved[4 * j + 2 + half, 32:] = second
+        return carry
+
+    lax.fori_loop(0, N // (2 * LANES), per_pair, 0, unroll=2)
+
+
+def first_rows_kernel(
+    offsets_in, distances_in, scales_in, beam_in, screen_in, twiddle_in, weight_in, moved,
+    field, table, l0, l1, l2, l3, r0, r1, r2, r3,
+    offsets, distances, scales, beam, screen, twiddle, weight, blocks, arrival, departure,
+):
+    pairs = (
+        (offsets_in, offsets), (distances_in, distances), (scales_in, scales),
+        (screen_in, screen), (beam_in, beam), (twiddle_in, twiddle), (weight_in, weight),
+    )
+    copies = [
+        pltpu.make_async_copy(source, target, arrival.at[i])
+        for i, (source, target) in enumerate(pairs)
+    ]
+    for copy in copies:
+        copy.start()
+    device = lax.axis_index(AXES)
+    for copy in copies[:2]:
+        copy.wait()
     transfer_table(table, distances[0], offsets[1])
+    for copy in copies[2:4]:
+        copy.wait()
+    pack_screen(scales, screen, blocks, device)
+
+    def leaving(part):
+        rows = slice(32, 64) if part == 4 else slice(8 * part, 8 * part + 8)
+        return pltpu.make_async_copy(blocks.at[:, rows], moved.at[:, rows], departure.at[part])
+
+    leaving(4).start()
+    for copy in copies[4:]:
+        copy.wait()
     low = low_half((8, LANES))
 
-    def rows_of(g):
-        return pl.ds(pl.multiple_of(g * 8, 8), 8)
-
     def first(g, carry):
-        rows = rows_of(g)
+        rows = eight_rows(g)
         for b in range(8):
             x = []
             for a in range(8):
@@ -268,60 +370,39 @@
         return carry
 
     lax.fori_loop(0, 4, first, 0)
-    spectral_pass(field, table, twiddle, weight, lhs, result, 32)
-
-    def last(g, carry):
-        rows = rows_of(g)
+    spectral_pass(field, table, twiddle, weight, (l0, l1, l2, l3), (r0, r1, r2, r3), 32)
+
+    def last(g):
+        rows = slice(8 * g, 8 * g + 8)
         for b in range(8):
             x = leave(field, b, rows)
             for a in range(8):
                 n1 = 8 * a + b
                 even, odd = swap_halves(x[a][0], x[a][1], low)
-                moved[2 * n1, rows] = even
-                moved[2 * n1 + 1, rows] = odd
-        return carry
-
-    lax.fori_loop(0, 4, last, 0)
+                blocks[2 * n1, rows] = even
+                blocks[2 * n1 + 1, rows] = odd
+        leaving(g).start()
+
+    for g in range(4):
+        last(g)
+    for part in range(5):
+        leaving(part).wait()
 
 
 def columns_kernel(
-    offsets, distances, scales, arrived, screen, twiddle, weight, moved,
-    field, table, lhs, result, turned, phases,
+    offsets, distances, arrived, twiddle, weight, moved,
+    field, table, l0, l1, l2, l3, r0, r1, r2, r3, turned,
 ):
-    device = lax.axis_index(AXES)
     transfer_table(table, distances[0], offsets[0])
-    lane = lax.broadcasted_iota(jnp.int32, (64, LANES), 1)
-
-    def screens(s, carry):
-        block = screen[pl.ds(pl.multiple_of(s * LANES, LANES), LANES), :].T
-        upper, lower = block[:64], block[64:]
-        upper32, lower32 = pltpu.roll(upper, 32, 1), pltpu.roll(lower, 32, 1)
-        upper64, lower64 = pltpu.roll(upper, 64, 1), pltpu.roll(lower, 64, 1)
-        upper96, lower96 = pltpu.roll(upper, 96, 1), pltpu.roll(lower, 96, 1)
-        even = jnp.where(
-            lane < 32, upper, jnp.where(lane < 64, lower32, jnp.where(lane < 96, upper32, lower64))
-        )
-        odd = jnp.where(
-            lane < 32, upper64, jnp.where(lane < 64, lower96, jnp.where(lane < 96, upper96, lower))
-        )
-        phases[2 * s] = even * scales[0, 2 * s, device // 2]
-        phases[2 * s + 1] = odd * scales[0, 2 * s + 1, device // 2]
-        return carry
-
-    lax.fori_loop(0, 32, screens, 0)
 
     def turn_in(n1, carry):
-        turned[n1] = arrived[pl.ds(pl.multiple_of(n1 * LANES, LANES), LANES), :].T
-        return carry
-
-    lax.fori_loop(0, 32, turn_in, 0)
-
-    def rows_of(g):
-        start = pl.multiple_of(g * 8, 8)
-        return pl.ds(start, 8), pl.ds(start + 64, 8)
+        turned[n1] = arrived[pl.ds(4 * n1, 4), :32].reshape((LANES, LANES)).T
+        return carry
+
+    lax.fori_loop(0, 32, turn_in, 0, unroll=4)
 
     def first(g, carry):
-        rows, rows_imag = rows_of(g)
+        rows, rows_imag = eight_rows(g), eight_rows(g + 8)
         for b in range(8):
             x = [
                 (turned[8 * a + b, rows], turned[8 * a + b, rows_imag]) if a < 4 else None
@@ -331,22 +412,28 @@
         return carry
 
     lax.fori_loop(0, 8, first, 0)
-    spectral_pass(field, table, twiddle, weight, lhs, result, 64)
+    spectral_pass(field, table, twiddle, weight, (l0, l1, l2, l3), (r0, r1, r2, r3), 64)
     transfer_table(table, distances[1], jnp.int32(0))
+    low = low_half((8, LANES))
 
     def middle(g, carry):
-        rows, _ = rows_of(g)
-        for b in range(8):
-            x = leave(field, b, rows)
-            x = [c_mul(x[a], sincos(phases[8 * a + b, rows])) for a in range(8)]
-            enter(field, b, rows, x)
-        return carry
-
-    lax.fori_loop(0, 8, middle, 0)
-    spectral_pass(field, table, twiddle, weight, lhs, result, 64)
+        for half in range(2):
+            rows = eight_rows(g + 4 * half)
+            for b in range(8):
+                x = leave(field, b, rows)
+                for a in range(8):
+                    n1 = 8 * a + b
+                    even, odd = arrived[2 * n1, eight_rows(g + 4)], arrived[2 * n1 + 1, eight_rows(g + 4)]
+                    turns = swap_halves(even, odd, low)[half]
+                    x[a] = c_mul(x[a], phasor(turns))
+                enter(field, b, rows, x)
+        return carry
+
+    lax.fori_loop(0, 4, middle, 0)
+    spectral_pass(field, table, twiddle, weight, (l0, l1, l2, l3), (r0, r1, r2, r3), 64)
 
     def last(g, carry):
-        rows, rows_imag = rows_of(g)
+        rows, rows_imag = eight_rows(g), eight_rows(g + 8)
         for b in range(8):
             x = leave(field, b, rows)
             for a in range(4):
@@ -360,21 +447,19 @@
         moved[pl.ds(pl.multiple_of(n1 * LANES, LANES), LANES), :] = turned[n1].T
         return carry
 
-    lax.fori_loop(0, 32, turn_out, 0)
+    lax.fori_loop(0, 32, turn_out, 0, unroll=4)
 
 
 def last_rows_kernel(
-    distances, scales, arrived, screen, twiddle, weight, output, field, table, lhs, result
+    distances, scales, arrived, screen, twiddle, weight, output,
+    field, table, l0, l1, l2, l3, r0, r1, r2, r3,
 ):
     device = lax.axis_index(AXES)
     transfer_table(table, distances[1], jnp.int32(0))
     low = low_half((8, LANES))
 
-    def rows_of(g):
-        return pl.ds(pl.multiple_of(g * 8, 8), 8)
-
     def first(g, carry):
-        rows = rows_of(g)
+        rows = eight_rows(g)
         for b in range(8):
             x = []
             for a in range(8):
@@ -384,17 +469,17 @@
         return carry
 
     lax.fori_loop(0, 4, first, 0)
-    spectral_pass(field, table, twiddle, weight, lhs, result, 32)
+    spectral_pass(field, table, twiddle, weight, (l0, l1, l2, l3), (r0, r1, r2, r3), 32)
 
     def last(g, carry):
-        rows = rows_of(g)
+        rows = eight_rows(g)
         for b in range(8):
             x = leave(field, b, rows)
             for a in range(4):
                 n1 = 8 * a + b
                 lanes = slice(n1 * LANES, (n1 + 1) * LANES)
-                phase = screen[rows, lanes].astype(F32) * scales[device // 4, n1]
-                value = c_mul(x[a + 2], sincos(phase))
+                scale = scales[device // 4, n1] * (0.5 / math.pi)
+                value = c_mul(x[a + 2], phasor(screen[rows, lanes].astype(F32) * scale))
                 output[0, rows, lanes] = value[0]
                 output[1, rows, lanes] = value[1]
         return carry
@@ -402,21 +487,21 @@
     lax.fori_loop(0, 4, last, 0)
 
 
-def call(kernel, kinds, shape, batch, extra, flops):
-    space = {"s": pltpu.SMEM, "v": pltpu.VMEM}
+def call(kernel, kinds, shape, batch, extra, flops, out_kind="v", limit=40):
+    space = {"s": pltpu.SMEM, "v": pltpu.VMEM, "h": pltpu.HBM}
     scratch = [
         pltpu.VMEM((2, 8, 8, batch, LANES), F32),
         pltpu.VMEM((2, 8, 8, LANES), F32),
-        pltpu.VMEM((8 * batch, 4 * LANES), BF16),
-        pltpu.VMEM((8 * batch, 2 * LANES), F32),
-    ] if batch else []
+        *[pltpu.VMEM((512, 4 * LANES), BF16)] * 4,
+        *[pltpu.VMEM((512, 2 * LANES), F32)] * 4,
+    ]
     return pl.pallas_call(
         kernel,
         out_shape=jax.ShapeDtypeStruct(shape, F32),
         in_specs=[pl.BlockSpec(memory_space=space[kind]) for kind in kinds],
-        out_specs=pl.BlockSpec(memory_space=pltpu.VMEM),
+        out_specs=pl.BlockSpec(memory_space=space[out_kind]),
         scratch_shapes=scratch + extra,
-        compiler_params=pltpu.CompilerParams(vmem_limit_bytes=48 << 20),
+        compiler_params=pltpu.CompilerParams(vmem_limit_bytes=limit << 20),
         cost_estimate=pl.CostEstimate(flops=flops, bytes_accessed=4 << 20, transcendentals=0),
     )
 
@@ -427,18 +512,28 @@
 
 def body(input_beam, offsets, distances, screens, screen_scales, last_screen, last_scales):
     twiddle, weight = (jnp.asarray(array) for array in constant_tables())
-    blocks = (128, 32, LANES)
-    packed = call(pack_screen_kernel, "v", blocks, 0, [], 1 << 20)(screens)
-    screen_columns = exchange(packed).reshape((4096, LANES))
-    moved = call(first_rows_kernel, "ssvvv", blocks, 32, [], 10**10)(
-        offsets, distances, input_beam, twiddle, weight
-    )
-    arrived = exchange(moved).reshape((4096, LANES))
-    extra = [pltpu.VMEM((32, LANES, LANES), F32), pltpu.VMEM((64, 64, LANES), F32)]
-    moved = call(columns_kernel, "sssvvvv", (4096, LANES), 64, extra, 4 * 10**10)(
-        offsets, distances, screen_scales, arrived, screen_columns, twiddle, weight
-    )
-    arrived = exchange(moved.reshape(blocks))
+    extra = [
+        pltpu.SMEM((2,), jnp.int32),
+        pltpu.SMEM((2,), F32),
+        pltpu.SMEM((1, 64, 64), F32),
+        pltpu.VMEM((2, 32, 4096), F32),
+        pltpu.VMEM((1, 64, N), jnp.int32),
+        pltpu.VMEM(twiddle.shape, F32),
+        pltpu.VMEM(weight.shape, BF16),
+        pltpu.VMEM((128, 64, LANES), F32),
+        pltpu.SemaphoreType.DMA((7,)),
+        pltpu.SemaphoreType.DMA((5,)),
+    ]
+    moved = call(
+        first_rows_kernel, "hhhhhhh", (128, 64, LANES), 32, extra, 10**10, "h", 60
+    )(
+        offsets, distances, screen_scales, input_beam, screens, twiddle, weight
+    )
+    extra = [pltpu.VMEM((32, LANES, LANES), F32)]
+    moved = call(columns_kernel, "ssvvv", (4096, LANES), 64, extra, 4 * 10**10)(
+        offsets, distances, exchange(moved), twiddle, weight
+    )
+    arrived = exchange(moved.reshape((128, 32, LANES)))
     return call(last_rows_kernel, "ssvvvv", (2, 32, 4096), 32, [], 10**10)(
         distances, last_scales, arrived, last_screen, twiddle, weight
     )

time: 174 us -> 142 us (0.82)
  blocking collectives: 69.7 us -> 102 us
  waiting for transfers between devices: 26.8 us -> 0 us
  Pallas kernels: 58.6 us -> 39.5 us
  starting transfers between devices: 11.9 us -> 0 us
  local copies, waits for them, and re-layouts: 6 us -> 0.04 us
    all_to_all x2, blocking collectives: 69.7 us -> 102 us  [exchange(): return lax.all_to_all(blocks, AXES, split_axis=0, concat_axis=0, tiled=True)]
    all_to_all x1 -> x0, waiting for transfers between devices: 26.8 us -> none  [exchange(): return lax.all_to_all(blocks, AXES, split_axis=0, concat_axis=0, tiled=True)]
    pallas_call x3 -> x2, Pallas kernels: 49.2 us -> 32.6 us  [the longest x1 22.8 us: body(): call(columns_kernel, 'ssvvv', (4096, LANES), 64, extra, 4 * 10 ** 10)]
    all_to_all x1 -> x0, starting transfers between devices: 11.9 us -> none  [exchange(): return lax.all_to_all(blocks, AXES, split_axis=0, concat_axis=0, tiled=True)]
    unnamed x26 -> x12, local copies, waits for them, and re-layouts: 6 us -> 0.04 us
    pallas_call x1, Pallas kernels: 9.41 us -> 6.96 us  [body(): call(last_rows_kernel, 'ssvvvv', (2, 32, 4096), 32, [], 10 ** 10)]
  transfers between devices with their start and end apart: 1 -> 0, of which waited for: 1 -> 0; matrix products, arithmetic and copies ran while one was open for 0% -> 0% of each run, Pallas kernels for 1% -> 0%
where the time goes in v2:
time: 142 us
  blocking collectives  102 us (72%)
  Pallas kernels  39.5 us (28%)
    all_to_all x2, blocking collectives, exchange(): return lax.all_to_all(blocks, AXES, split_axis=0, concat_axis=0, tiled=True)  102 us
    pallas_call x1, Pallas kernels, body(): call(columns_kernel, 'ssvvv', (4096, LANES), 64, extra, 4 * 10 ** 10)  22.8 us
    pallas_call x1, Pallas kernels, body(): call(first_rows_kernel, 'hhhhhhh', (128, 64, LANES), 32, extra, 10 ** 10,...  9.81 us
    pallas_call x1, Pallas kernels, body(): call(last_rows_kernel, 'ssvvvv', (2, 32, 4096), 32, [], 10 ** 10)  6.96 us

profile of v2, /device:TPU:1, one launch (start us, length us, event | category | flops | bytes accessed | tf_op | source)
XLA Modules:
  0.0 141.8 jit_solution(18007617019358642443)
XLA Ops:
  0.0 9.8 %shard_map.91 = f32[128,64,128]{2,1,0:T(8,128)} custom-call(s32[2]{0:T(128)} %offsets.1, f32[2]{0:T(128)} %distances.3, f32[1,64,64]{2,1,0:T(8,128)} %scales_in.1, f32[2,32,4096]{2,1,0:T(8,128)} %beam_in.1, s32[1,64,8192]{2,1,0:T(8,128)} %screen_in.1, f32[2,8,8,128]{3,2,1,0:T(8,128)} %constant.4.clone.twiddle_in.twiddle, ...), custom_call_target="tpu_custom_call" | custom-call | flops 10000000000 | bytes 4194304 | tf_op jit(solution)/shard_map/pallas_call | solution.py:527
  9.8 0.0 copy-start.2
  9.8 0.0 copy-start.3
  9.8 0.0 copy-start.4
  9.9 0.0 copy-start.5
  9.9 64.2 %all_to_all.10.arrived = f32[128,64,128]{2,1,0:T(8,128)S(1)} all-to-all(f32[128,64,128]{2,1,0:T(8,128)} %shard_map.91), channel_id=1, replica_groups=mesh['gx'=8,'gy'=16] {'gx','gy'}, dimensions={0} | all-to-all | bytes 8388608 | tf_op jit(solution)/shard_map/all_to_all | solution.py:510
  74.1 0.0 copy-done.2
  74.1 0.0 copy-done.3
  74.1 0.0 copy-done.4
  74.1 0.0 copy-done.5
  74.1 22.8 %shard_map.92 = f32[4096,128]{1,0:T(8,128)S(1)} custom-call(s32[2]{0:T(128)S(1)} %copy-done.2, f32[2]{0:T(128)S(1)} %copy-done.3, f32[128,64,128]{2,1,0:T(8,128)S(1)} %all_to_all.10.arrived, f32[2,8,8,128]{3,2,1,0:T(8,128)S(1)} %copy-done.5, bf16[768,256]{1,0:T(8,128)(2,1)S(1)} %copy-done.4), custom_call_target="tpu_custom_call" | custom-call | flops 40000000000 | bytes 4194304 | tf_op jit(solution)/shard_map/pallas_call | solution.py:533
  96.9 0.0 copy-start
  96.9 0.0 copy-start.1
  96.9 37.9 %all_to_all.11.arrived = f32[128,32,128]{2,1,0:T(8,128)S(1)} all-to-all(f32[128,32,128]{2,1,0:T(8,128)S(1)} %bitcast.1), channel_id=1, replica_groups=mesh['gx'=8,'gy'=16] {'gx','gy'}, dimensions={0} | all-to-all | bytes 4194304 | tf_op jit(solution)/shard_map/all_to_all | solution.py:510
  134.8 0.0 copy-done
  134.8 0.0 copy-done.1
  134.8 7.0 %shard_map.93 = f32[2,32,4096]{2,1,0:T(8,128)} custom-call(f32[2]{0:T(128)S(1)} %copy-done.3, f32[32,32]{1,0:T(8,128)S(1)} %copy-done.1, f32[128,32,128]{2,1,0:T(8,128)S(1)} %all_to_all.11.arrived, s32[32,4096]{1,0:T(8,128)S(1)} %copy-done, f32[2,8,8,128]{3,2,1,0:T(8,128)S(1)} %copy-done.5, bf16[768,256]{1,0:T(8,128)(2,1)S(1)} %copy-done.4), custom_call_target="tpu_custom_call" | custom-call | flops 10000000000 | bytes 4194304 | tf_op jit(solution)/shard_map/pallas_call | solution.py:537
Async XLA Ops:
  9.8 64.3 %copy-start.2 = (s32[2]{0:T(128)S(1)}, s32[2]{0:T(128)}, u32[]{:S(2)}) copy-start(s32[2]{0:T(128)} %offsets.1) | copy-start | bytes 28
  9.8 64.3 %copy-start.3 = (f32[2]{0:T(128)S(1)}, f32[2]{0:T(128)}, u32[]{:S(2)}) copy-start(f32[2]{0:T(128)} %distances.3) | copy-start | bytes 28
  9.8 64.3 %copy-start.4 = (bf16[768,256]{1,0:T(8,128)(2,1)S(1)}, bf16[768,256]{1,0:T(8,128)(2,1)}, u32[]{:S(2)}) copy-start(bf16[768,256]{1,0:T(8,128)(2,1)} %constant.5.clone.weight_in.weight) | copy-start | bytes 1179652
  9.9 64.2 %copy-start.5 = (f32[2,8,8,128]{3,2,1,0:T(8,128)S(1)}, f32[2,8,8,128]{3,2,1,0:T(8,128)}, u32[]{:S(2)}) copy-start(f32[2,8,8,128]{3,2,1,0:T(8,128)} %constant.4.clone.twiddle_in.twiddle) | copy-start | bytes 196612
  96.9 37.9 %copy-start = (s32[32,4096]{1,0:T(8,128)S(1)}, s32[32,4096]{1,0:T(8,128)}, u32[]{:S(2)}) copy-start(s32[32,4096]{1,0:T(8,128)} %screen.1) | copy-start | bytes 1572868
  96.9 37.9 %copy-start.1 = (f32[32,32]{1,0:T(8,128)S(1)}, f32[32,32]{1,0:T(8,128)}, u32[]{:S(2)}) copy-start(f32[32,32]{1,0:T(8,128)} %scales.1) | copy-start | bytes 12292

commit v3 on v2

--- a/solution.py
+++ b/solution.py
@@ -147,7 +147,7 @@
     return 1.0 - sine * sine, sine * cosine
 
 
-def transfer_table(table, distance, offset):
+def transfer_table(table, at, distance, offset):
     shape = (8, LANES)
     q_ids = lax.broadcasted_iota(jnp.int32, shape, 0)
     lane_ids = lax.broadcasted_iota(jnp.int32, shape, 1)
@@ -169,8 +169,8 @@
         ramp = (k * offset) & (N - 1)
         ramp = jnp.where(ramp < N // 2, ramp, ramp - N).astype(F32) * (2.0 * math.pi / N)
         cosine, sine = sincos(rest + ramp)
-        table[0, p] = cosine * (1.0 / N)
-        table[1, p] = sine * (-1.0 / N)
+        table[at, 0, p] = cosine * (1.0 / N)
+        table[at, 1, p] = sine * (-1.0 / N)
 
 
 def split_pair(first, second):
@@ -195,13 +195,17 @@
     )
 
 
-def spectral_pass(field, table, twiddle, weight, left, result, batch):
+def spectral_pass(field, table, twiddle, weight, left, result, batch, side=None):
     groups = batch // 8
     width = 64 // batch
     steps = 8 // width
 
     def row_of(values, part, p, q):
         return values[part, p, q : q + 1, :]
+
+    def table_row(part, p, q):
+        values, at = table
+        return values[at, part, p, q : q + 1, :]
 
     def places(step):
         for j in range(width):
@@ -212,7 +216,9 @@
         return slice(row + 8 * q, row + 8 * q + 8)
 
     def forward(step, lhs):
-        for p, rows, row in places(step):
+        for i, (p, rows, row) in enumerate(places(step)):
+            if side is not None:
+                side(step, i)
             x = radix8([(field[0, p, b, rows], field[1, p, b, rows]) for b in range(8)], -1)
             x = [
                 c_mul(x[q], (row_of(twiddle, 0, p, q), row_of(twiddle, 1, p, q)))
@@ -227,7 +233,7 @@
             for q in range(8):
                 at = result_rows(row, q)
                 value = (values[at, :LANES], values[at, LANES:])
-                x.append(c_mul(value, (row_of(table, 0, p, q), row_of(table, 1, p, q))))
+                x.append(c_mul(value, (table_row(0, p, q), table_row(1, p, q))))
             store_split(lhs, row, [v[1] for v in x], 0)
             store_split(lhs, row, [v[0] for v in x], LANES)
 
@@ -258,7 +264,7 @@
     multiply(inverse_left[0], inverse_result[0])
     forward(2, forward_left[0])
 
-    def two_steps(i, carry):
+    def two_steps(i, carry, more=True):
         step = 2 * i
         multiply(forward_left[0], forward_result[0])
         transfer(step - 1, forward_result[1], inverse_left[1])
@@ -269,10 +275,13 @@
         transfer(step, forward_result[0], inverse_left[0])
         multiply(inverse_left[0], inverse_result[0])
         inverse(step - 1, inverse_result[1])
-        forward(jnp.minimum(step + 2, steps - 1), forward_left[0])
+        if more:
+            forward(step + 2, forward_left[0])
         return carry
 
-    lax.fori_loop(1, steps // 2, two_steps, 0)
+    if steps > 4:
+        lax.fori_loop(1, steps // 2 - 1, two_steps, 0)
+    two_steps(steps // 2 - 1, 0, more=False)
     transfer(steps - 1, forward_result[1], inverse_left[1])
     multiply(inverse_left[1], inverse_result[1])
     inverse(steps - 2, inverse_result[0])
@@ -303,37 +312,32 @@
 
 
 def eight_rows(g):
-    return pl.ds(pl.multiple_of(g * 8, 8), 8)
-
-
-def pack_screen(scales, screen, moved, device):
-    low = low_half((32, LANES))
-
-    def per_pair(j, carry):
-        tiles = []
-        for half in range(2):
-            lanes = pl.ds(pl.multiple_of(j * (2 * LANES), 2 * LANES) + half * LANES, LANES)
-            scale = scales[0, device // 2, 2 * j + half] * (0.5 / math.pi)
-            tiles.append(screen[0, :, lanes].astype(F32) * scale)
-        block = jnp.concatenate(tiles, axis=0).T
-        for half in range(2):
-            part = block[64 * half : 64 * half + 64]
-            first, second = swap_halves(part[:32], part[32:], low)
-            moved[4 * j + half, 32:] = first
-            moved[4 * j + 2 + half, 32:] = second
-        return carry
-
-    lax.fori_loop(0, N // (2 * LANES), per_pair, 0, unroll=2)
+    return pl.ds(g * 8 if isinstance(g, int) else pl.multiple_of(g * 8, 8), 8)
+
+
+def pack_screen(j, scales, screen, moved, device, low):
+    tiles = []
+    for half in range(2):
+        start = j * (2 * LANES) + half * LANES
+        lanes = pl.ds(start if isinstance(j, int) else pl.multiple_of(start, LANES), LANES)
+        scale = scales[0, device // 2, 2 * j + half] * (0.5 / math.pi)
+        tiles.append(screen[0, :, lanes].astype(F32) * scale)
+    block = jnp.concatenate(tiles, axis=0).T
+    for half in range(2):
+        part = block[64 * half : 64 * half + 64]
+        first, second = swap_halves(part[:32], part[32:], low)
+        moved[4 * j + half, 32:] = first
+        moved[4 * j + 2 + half, 32:] = second
 
 
 def first_rows_kernel(
     offsets_in, distances_in, scales_in, beam_in, screen_in, twiddle_in, weight_in, moved,
-    field, table, l0, l1, l2, l3, r0, r1, r2, r3,
+    field, l0, l1, l2, l3, r0, r1, r2, r3, table,
     offsets, distances, scales, beam, screen, twiddle, weight, blocks, arrival, departure,
 ):
     pairs = (
         (offsets_in, offsets), (distances_in, distances), (scales_in, scales),
-        (screen_in, screen), (beam_in, beam), (twiddle_in, twiddle), (weight_in, weight),
+        (beam_in, beam), (twiddle_in, twiddle), (weight_in, weight), (screen_in, screen),
     )
     copies = [
         pltpu.make_async_copy(source, target, arrival.at[i])
@@ -344,18 +348,13 @@
     device = lax.axis_index(AXES)
     for copy in copies[:2]:
         copy.wait()
-    transfer_table(table, distances[0], offsets[1])
-    for copy in copies[2:4]:
-        copy.wait()
-    pack_screen(scales, screen, blocks, device)
+    transfer_table(table, 0, distances[0], offsets[1])
+    copies[3].wait()
 
     def leaving(part):
         rows = slice(32, 64) if part == 4 else slice(8 * part, 8 * part + 8)
         return pltpu.make_async_copy(blocks.at[:, rows], moved.at[:, rows], departure.at[part])
 
-    leaving(4).start()
-    for copy in copies[4:]:
-        copy.wait()
     low = low_half((8, LANES))
 
     def first(g, carry):
@@ -370,7 +369,14 @@
         return carry
 
     lax.fori_loop(0, 4, first, 0)
-    spectral_pass(field, table, twiddle, weight, (l0, l1, l2, l3), (r0, r1, r2, r3), 32)
+    for copy in (copies[2], *copies[4:]):
+        copy.wait()
+    low_packed = low_half((32, LANES))
+    spectral_pass(
+        field, (table, 0), twiddle, weight, (l0, l1, l2, l3), (r0, r1, r2, r3), 32,
+        lambda step, i: pack_screen(8 * step + i, scales, screen, blocks, device, low_packed),
+    )
+    leaving(4).start()
 
     def last(g):
         rows = slice(8 * g, 8 * g + 8)
@@ -389,73 +395,113 @@
         leaving(part).wait()
 
 
+def tables_kernel(offsets, distances, scales, screen, moved, tables, phasors):
+    del moved
+    device = lax.axis_index(AXES)
+    transfer_table(tables, 0, distances[0], offsets[0])
+    transfer_table(tables, 1, distances[1], jnp.int32(0))
+
+    def tiles(j, carry):
+        for i in range(4):
+            n1 = 4 * j + i
+            lanes = pl.ds(pl.multiple_of(n1 * LANES, LANES), LANES)
+            scale = scales[device // 4, n1] * (0.5 / math.pi)
+            phasors[0, :, lanes], phasors[1, :, lanes] = phasor(
+                screen[:, lanes].astype(F32) * scale
+            )
+        return carry
+
+    lax.fori_loop(0, 8, tiles, 0)
+
+
 def columns_kernel(
-    offsets, distances, arrived, twiddle, weight, moved,
-    field, table, l0, l1, l2, l3, r0, r1, r2, r3, turned,
+    arrived_in, tables_in, twiddle_in, weight_in, moved,
+    field, l0, l1, l2, l3, r0, r1, r2, r3,
+    turned, arrived, tables, twiddle, weight, blocks, arrival, departure,
 ):
-    transfer_table(table, distances[0], offsets[0])
-
-    def turn_in(n1, carry):
-        turned[n1] = arrived[pl.ds(4 * n1, 4), :32].reshape((LANES, LANES)).T
-        return carry
-
-    lax.fori_loop(0, 32, turn_in, 0, unroll=4)
-
-    def first(g, carry):
-        rows, rows_imag = eight_rows(g), eight_rows(g + 8)
-        for b in range(8):
-            x = [
-                (turned[8 * a + b, rows], turned[8 * a + b, rows_imag]) if a < 4 else None
-                for a in range(8)
-            ]
-            enter(field, b, rows, x)
-        return carry
-
-    lax.fori_loop(0, 8, first, 0)
-    spectral_pass(field, table, twiddle, weight, (l0, l1, l2, l3), (r0, r1, r2, r3), 64)
-    transfer_table(table, distances[1], jnp.int32(0))
+    constants = [
+        pltpu.make_async_copy(source, target, arrival.at[33 + i])
+        for i, (source, target) in enumerate(
+            ((tables_in, tables), (twiddle_in, twiddle), (weight_in, weight))
+        )
+    ]
+
+    def copy_of(n1):
+        part = slice(4 * n1, 4 * n1 + 4), slice(0, 32)
+        if n1 == 32:
+            part = slice(0, 128), slice(32, 64)
+        return pltpu.make_async_copy(arrived_in.at[part], arrived.at[part], arrival.at[n1])
+
+    for b in range(8):
+        for a in range(4):
+            copy_of(8 * a + b).start()
+    for copy in constants:
+        copy.start()
+    copy_of(32).start()
+
+    def leaving(n1):
+        rows = slice(n1 * LANES, (n1 + 1) * LANES)
+        return pltpu.make_async_copy(blocks.at[rows], moved.at[rows], departure.at[n1])
+
+    def turned_rows(slot, g):
+        return turned.at[slot, 8 * g : 8 * g + 8], turned.at[slot, 8 * g + 64 : 8 * g + 72]
+
+    for b in range(8):
+        slots = [a + 4 * (b % 2) for a in range(4)]
+        for a in range(4):
+            copy_of(8 * a + b).wait()
+        for a in range(4):
+            n1 = 8 * a + b
+            turned[slots[a]] = arrived[4 * n1 : 4 * n1 + 4, :32].reshape((LANES, LANES)).T
+        for g in range(8):
+            x = []
+            for slot in slots:
+                real, imag = turned_rows(slot, g)
+                x.append((real[...], imag[...]))
+            enter(field, b, slice(8 * g, 8 * g + 8), x + [None] * 4)
+
+    for copy in constants:
+        copy.wait()
+    buffers = (l0, l1, l2, l3), (r0, r1, r2, r3)
+    spectral_pass(field, (tables, 0), twiddle, weight, *buffers, 64)
+    copy_of(32).wait()
     low = low_half((8, LANES))
 
     def middle(g, carry):
         for half in range(2):
             rows = eight_rows(g + 4 * half)
+            packed = eight_rows(g + 4)
             for b in range(8):
                 x = leave(field, b, rows)
                 for a in range(8):
                     n1 = 8 * a + b
-                    even, odd = arrived[2 * n1, eight_rows(g + 4)], arrived[2 * n1 + 1, eight_rows(g + 4)]
-                    turns = swap_halves(even, odd, low)[half]
-                    x[a] = c_mul(x[a], phasor(turns))
+                    even, odd = arrived[2 * n1, packed], arrived[2 * n1 + 1, packed]
+                    x[a] = c_mul(x[a], phasor(swap_halves(even, odd, low)[half]))
                 enter(field, b, rows, x)
         return carry
 
     lax.fori_loop(0, 4, middle, 0)
-    spectral_pass(field, table, twiddle, weight, (l0, l1, l2, l3), (r0, r1, r2, r3), 64)
-
-    def last(g, carry):
-        rows, rows_imag = eight_rows(g), eight_rows(g + 8)
-        for b in range(8):
-            x = leave(field, b, rows)
+    spectral_pass(field, (tables, 1), twiddle, weight, *buffers, 64)
+
+    for b in range(8):
+        slots = [a + 4 * (b % 2) for a in range(4)]
+        for g in range(8):
+            x = leave(field, b, slice(8 * g, 8 * g + 8))
             for a in range(4):
-                turned[8 * a + b, rows] = x[a + 2][0]
-                turned[8 * a + b, rows_imag] = x[a + 2][1]
-        return carry
-
-    lax.fori_loop(0, 8, last, 0)
-
-    def turn_out(n1, carry):
-        moved[pl.ds(pl.multiple_of(n1 * LANES, LANES), LANES), :] = turned[n1].T
-        return carry
-
-    lax.fori_loop(0, 32, turn_out, 0, unroll=4)
+                real, imag = turned_rows(slots[a], g)
+                real[...], imag[...] = x[a + 2]
+        for a in range(4):
+            n1 = 8 * a + b
+            blocks[n1 * LANES : (n1 + 1) * LANES, :] = turned[slots[a]].T
+            leaving(n1).start()
+    for n1 in range(32):
+        leaving(n1).wait()
 
 
 def last_rows_kernel(
-    distances, scales, arrived, screen, twiddle, weight, output,
-    field, table, l0, l1, l2, l3, r0, r1, r2, r3,
+    arrived, tables, phasors, twiddle, weight, output_in_hbm,
+    field, l0, l1, l2, l3, r0, r1, r2, r3, output, departure,
 ):
-    device = lax.axis_index(AXES)
-    transfer_table(table, distances[1], jnp.int32(0))
     low = low_half((8, LANES))
 
     def first(g, carry):
@@ -469,7 +515,7 @@
         return carry
 
     lax.fori_loop(0, 4, first, 0)
-    spectral_pass(field, table, twiddle, weight, (l0, l1, l2, l3), (r0, r1, r2, r3), 32)
+    spectral_pass(field, (tables, 1), twiddle, weight, (l0, l1, l2, l3), (r0, r1, r2, r3), 32)
 
     def last(g, carry):
         rows = eight_rows(g)
@@ -478,28 +524,35 @@
             for a in range(4):
                 n1 = 8 * a + b
                 lanes = slice(n1 * LANES, (n1 + 1) * LANES)
-                scale = scales[device // 4, n1] * (0.5 / math.pi)
-                value = c_mul(x[a + 2], phasor(screen[rows, lanes].astype(F32) * scale))
+                value = c_mul(x[a + 2], (phasors[0, rows, lanes], phasors[1, rows, lanes]))
                 output[0, rows, lanes] = value[0]
                 output[1, rows, lanes] = value[1]
+        leaving(g).start()
         return carry
 
+    def leaving(g):
+        rows = eight_rows(g)
+        return pltpu.make_async_copy(
+            output.at[:, rows], output_in_hbm.at[:, rows], departure.at[g]
+        )
+
     lax.fori_loop(0, 4, last, 0)
-
-
-def call(kernel, kinds, shape, batch, extra, flops, out_kind="v", limit=40):
+    for g in range(4):
+        leaving(g).wait()
+
+
+def call(kernel, kinds, shapes, batch, extra, flops, out_kind="v", limit=40):
     space = {"s": pltpu.SMEM, "v": pltpu.VMEM, "h": pltpu.HBM}
     scratch = [
         pltpu.VMEM((2, 8, 8, batch, LANES), F32),
-        pltpu.VMEM((2, 8, 8, LANES), F32),
         *[pltpu.VMEM((512, 4 * LANES), BF16)] * 4,
         *[pltpu.VMEM((512, 2 * LANES), F32)] * 4,
-    ]
+    ] if batch else []
     return pl.pallas_call(
         kernel,
-        out_shape=jax.ShapeDtypeStruct(shape, F32),
+        out_shape=[jax.ShapeDtypeStruct(shape, F32) for shape in shapes],
         in_specs=[pl.BlockSpec(memory_space=space[kind]) for kind in kinds],
-        out_specs=pl.BlockSpec(memory_space=space[out_kind]),
+        out_specs=[pl.BlockSpec(memory_space=space[out_kind]) for _ in shapes],
         scratch_shapes=scratch + extra,
         compiler_params=pltpu.CompilerParams(vmem_limit_bytes=limit << 20),
         cost_estimate=pl.CostEstimate(flops=flops, bytes_accessed=4 << 20, transcendentals=0),
@@ -512,7 +565,9 @@
 
 def body(input_beam, offsets, distances, screens, screen_scales, last_screen, last_scales):
     twiddle, weight = (jnp.asarray(array) for array in constant_tables())
+    table = (2, 8, 8, LANES)
     extra = [
+        pltpu.VMEM((1, *table), F32),
         pltpu.SMEM((2,), jnp.int32),
         pltpu.SMEM((2,), F32),
         pltpu.SMEM((1, 64, 64), F32),
@@ -524,19 +579,31 @@
         pltpu.SemaphoreType.DMA((7,)),
         pltpu.SemaphoreType.DMA((5,)),
     ]
-    moved = call(
-        first_rows_kernel, "hhhhhhh", (128, 64, LANES), 32, extra, 10**10, "h", 60
-    )(
-        offsets, distances, screen_scales, input_beam, screens, twiddle, weight
-    )
-    extra = [pltpu.VMEM((32, LANES, LANES), F32)]
-    moved = call(columns_kernel, "ssvvv", (4096, LANES), 64, extra, 4 * 10**10)(
-        offsets, distances, exchange(moved), twiddle, weight
-    )
+    (moved,) = call(
+        first_rows_kernel, "hhhhhhh", [(128, 64, LANES)], 32, extra, 10**10, "h", 60
+    )(offsets, distances, screen_scales, input_beam, screens, twiddle, weight)
+    tables, phasors = call(
+        tables_kernel, "sssvh", [(2, *table), (2, 32, 4096)], 0, [], 10**9, "v", 60
+    )(offsets, distances, last_scales, last_screen, moved)
+    extra = [
+        pltpu.VMEM((8, LANES, LANES), F32),
+        pltpu.VMEM((128, 64, LANES), F32),
+        pltpu.VMEM((2, *table), F32),
+        pltpu.VMEM(twiddle.shape, F32),
+        pltpu.VMEM(weight.shape, BF16),
+        pltpu.VMEM((4096, LANES), F32),
+        pltpu.SemaphoreType.DMA((36,)),
+        pltpu.SemaphoreType.DMA((32,)),
+    ]
+    (moved,) = call(
+        columns_kernel, "hhhh", [(4096, LANES)], 64, extra, 4 * 10**10, "h", 60
+    )(exchange(moved), tables, twiddle, weight)
     arrived = exchange(moved.reshape((128, 32, LANES)))
-    return call(last_rows_kernel, "ssvvvv", (2, 32, 4096), 32, [], 10**10)(
-        distances, last_scales, arrived, last_screen, twiddle, weight
-    )
+    extra = [pltpu.VMEM((2, 32, 4096), F32), pltpu.SemaphoreType.DMA((4,))]
+    (output,) = call(last_rows_kernel, "vvvvv", [(2, 32, 4096)], 32, extra, 10**10, "h")(
+        arrived, tables, phasors, twiddle, weight
+    )
+    return output
 
 
 def solution(mesh):

time: 142 us -> 138 us (0.972)
  blocking collectives: 102 us -> 38.1 us
  waiting for transfers between devices: 0 us -> 49.6 us
  starting transfers between devices: 0 us -> 12 us
  Pallas kernels: 39.5 us -> 37.7 us
    all_to_all x2 -> x1, blocking collectives: 102 us -> 38.1 us  [exchange(): return lax.all_to_all(blocks, AXES, split_axis=0, concat_axis=0, tiled=True)]
    all_to_all x0 -> x1, waiting for transfers between devices: none -> 49.6 us  [exchange(): return lax.all_to_all(blocks, AXES, split_axis=0, concat_axis=0, tiled=True)]
    all_to_all x0 -> x1, starting transfers between devices: none -> 12 us  [exchange(): return lax.all_to_all(blocks, AXES, split_axis=0, concat_axis=0, tiled=True)]
    pallas_call x3 -> x4, Pallas kernels: 39.5 us -> 37.7 us  [the longest x1 22.4 us: body(): call(columns_kernel, 'hhhh', [(4096, LANES)], 64, extra, 4 * 10 ** 10, 'h...]
  transfers between devices with their start and end apart: 0 -> 1, of which waited for: 0 -> 1; matrix products, arithmetic and copies ran while one was open for 0% -> 0% of each run, Pallas kernels for 0% -> 2%
where the time goes in v3:
time: 138 us
  waiting for transfers between devices  49.6 us (36%)
  blocking collectives  38.1 us (28%)
  Pallas kernels  37.7 us (27%)
  starting transfers between devices  12 us (9%)
    all_to_all x1, waiting for transfers between devices, exchange(): return lax.all_to_all(blocks, AXES, split_axis=0, concat_axis=0, tiled=True)  49.6 us
    all_to_all x1, blocking collectives, exchange(): return lax.all_to_all(blocks, AXES, split_axis=0, concat_axis=0, tiled=True)  38.1 us
    pallas_call x1, Pallas kernels, body(): call(columns_kernel, 'hhhh', [(4096, LANES)], 64, extra, 4 * 10 ** 10, 'h...  22.4 us
    all_to_all x1, starting transfers between devices, exchange(): return lax.all_to_all(blocks, AXES, split_axis=0, concat_axis=0, tiled=True)  12 us
    pallas_call x1, Pallas kernels, body(): call(first_rows_kernel, 'hhhhhhh', [(128, 64, LANES)], 32, extra, 10 ** 1...  7.28 us
    pallas_call x1, Pallas kernels, body(): call(last_rows_kernel, 'vvvvv', [(2, 32, 4096)], 32, extra, 10 ** 10, 'h')  5.29 us
    pallas_call x1, Pallas kernels, body(): call(tables_kernel, 'sssvh', [(2, *table), (2, 32, 4096)], 0, [], 10 ** 9...  2.79 us
  transfers between devices with their start and end apart: 1, of which 1 were waited for; matrix products, arithmetic and copies ran while one was open for 0% of the time, Pallas kernels for 2%

profile of v3, /device:TPU:1, one launch (start us, length us, event | category | flops | bytes accessed | tf_op | source)
XLA Modules:
  0.0 137.7 jit_solution(16268885896908256655)
XLA Ops:
  0.0 7.3 %shard_map.91.moved = f32[128,64,128]{2,1,0:T(8,128)} custom-call(s32[2]{0:T(128)} %offsets.1, f32[2]{0:T(128)} %distances.1, f32[1,64,64]{2,1,0:T(8,128)} %scales_in.1, f32[2,32,4096]{2,1,0:T(8,128)} %beam_in.1, s32[1,64,8192]{2,1,0:T(8,128)} %screen_in.1, f32[2,8,8,128]{3,2,1,0:T(8,128)} %constant.4.clone.twiddle_in.twiddle, ...), custom_call_target="tpu_custom_call" | custom-call | flops 10000000000 | bytes 4194304 | tf_op jit(solution)/shard_map/pallas_call | solution.py:582
  7.3 12.0 %all-to-all-start = ((f32[128,64,128]{2,1,0:T(8,128)}), f32[128,64,128]{2,1,0:T(8,128)}, u32[]{:S(2)}, u32[]{:S(2)}) async-start(f32[128,64,128]{2,1,0:T(8,128)} %shard_map.91.moved), calls=%async_computation | async-start | bytes 8388608 | tf_op jit(solution)/shard_map/all_to_all | solution.py:563
  19.3 2.8 %shard_map.92 = (f32[2,2,8,8,128]{4,3,2,1,0:T(8,128)}, f32[2,32,4096]{2,1,0:T(8,128)}) custom-call(s32[2]{0:T(128)} %offsets.1, f32[2]{0:T(128)} %distances.1, f32[32,32]{1,0:T(8,128)} %scales.1, s32[32,4096]{1,0:T(8,128)} %screen.1, f32[128,64,128]{2,1,0:T(8,128)} %shard_map.91.moved), custom_call_target="tpu_custom_call" | custom-call | flops 1000000000 | bytes 4194304 | tf_op jit(solution)/shard_map/pallas_call | solution.py:585
  22.1 49.6 %all-to-all-done.arrived_in = f32[128,64,128]{2,1,0:T(8,128)} async-done(((f32[128,64,128]{2,1,0:T(8,128)}), f32[128,64,128]{2,1,0:T(8,128)}, u32[]{:S(2)}, u32[]{:S(2)}) %all-to-all-start) | async-done | bytes 4194336 | tf_op jit(solution)/shard_map/all_to_all | solution.py:563
  71.6 22.4 %shard_map.93 = f32[4096,128]{1,0:T(8,128)} custom-call(f32[128,64,128]{2,1,0:T(8,128)} %all-to-all-done.arrived_in, f32[2,2,8,8,128]{4,3,2,1,0:T(8,128)} %get-tuple-element.7.tables_in.tables, f32[2,8,8,128]{3,2,1,0:T(8,128)} %constant.4.clone.twiddle_in.twiddle, bf16[768,256]{1,0:T(8,128)(2,1)} %constant.5.clone.weight_in.weight), custom_call_target="tpu_custom_call" | custom-call | flops 40000000000 | bytes 4194304 | tf_op jit(solution)/shard_map/pallas_call | solution.py:598
  94.0 0.0 copy-start
  94.0 0.0 copy-start.1
  94.0 0.0 copy-start.2
  94.0 0.0 copy-start.3
  94.0 38.1 %all_to_all.10.arrived = f32[128,32,128]{2,1,0:T(8,128)S(1)} all-to-all(f32[128,32,128]{2,1,0:T(8,128)} %bitcast.1), channel_id=1, replica_groups=mesh['gx'=8,'gy'=16] {'gx','gy'}, dimensions={0} | all-to-all | bytes 4194304 | tf_op jit(solution)/shard_map/all_to_all | solution.py:563
  132.2 0.0 copy-done
  132.2 0.0 copy-done.1
  132.2 0.0 copy-done.2
  132.2 0.0 copy-done.3
  132.2 5.3 %shard_map.94 = f32[2,32,4096]{2,1,0:T(8,128)} custom-call(f32[128,32,128]{2,1,0:T(8,128)S(1)} %all_to_all.10.arrived, f32[2,2,8,8,128]{4,3,2,1,0:T(8,128)S(1)} %copy-done.1, f32[2,32,4096]{2,1,0:T(8,128)S(1)} %copy-done, f32[2,8,8,128]{3,2,1,0:T(8,128)S(1)} %copy-done.3, bf16[768,256]{1,0:T(8,128)(2,1)S(1)} %copy-done.2), custom_call_target="tpu_custom_call" | custom-call | flops 10000000000 | bytes 4194304 | tf_op jit(solution)/shard_map/pallas_call | solution.py:603
Async XLA Ops:
  7.3 64.3 %all-to-all-start = ((f32[128,64,128]{2,1,0:T(8,128)}), f32[128,64,128]{2,1,0:T(8,128)}, u32[]{:S(2)}, u32[]{:S(2)}) async-start(f32[128,64,128]{2,1,0:T(8,128)} %shard_map.91.moved), calls=%async_computation | async-start | bytes 8388608 | tf_op jit(solution)/shard_map/all_to_all | solution.py:563
  94.0 38.2 %copy-start = (f32[2,32,4096]{2,1,0:T(8,128)S(1)}, f32[2,32,4096]{2,1,0:T(8,128)}, u32[]{:S(2)}) copy-start(f32[2,32,4096]{2,1,0:T(8,128)} %get-tuple-element.8.phasors) | copy-start | bytes 3145732
  94.0 38.2 %copy-start.1 = (f32[2,2,8,8,128]{4,3,2,1,0:T(8,128)S(1)}, f32[2,2,8,8,128]{4,3,2,1,0:T(8,128)}, u32[]{:S(2)}) copy-start(f32[2,2,8,8,128]{4,3,2,1,0:T(8,128)} %get-tuple-element.7.tables_in.tables) | copy-start | bytes 393220
  94.0 38.2 %copy-start.2 = (bf16[768,256]{1,0:T(8,128)(2,1)S(1)}, bf16[768,256]{1,0:T(8,128)(2,1)}, u32[]{:S(2)}) copy-start(bf16[768,256]{1,0:T(8,128)(2,1)} %constant.5.clone.weight_in.weight) | copy-start | bytes 1179652
  94.0 38.2 %copy-start.3 = (f32[2,8,8,128]{3,2,1,0:T(8,128)S(1)}, f32[2,8,8,128]{3,2,1,0:T(8,128)}, u32[]{:S(2)}) copy-start(f32[2,8,8,128]{3,2,1,0:T(8,128)} %constant.4.clone.twiddle_in.twiddle) | copy-start | bytes 196612

commit v4 on v3

--- a/solution.py
+++ b/solution.py
@@ -173,19 +173,14 @@
         table[at, 1, p] = sine * (-1.0 / N)
 
 
-def split_pair(first, second):
-    both = jnp.concatenate([first, second], axis=0)
-    high = both.astype(BF16)
-    low = (both - high.astype(F32)).astype(BF16)
-    return high, low
-
-
-def store_split(lhs, row, values, lane):
-    for half in range(4):
-        high, low = split_pair(values[2 * half], values[2 * half + 1])
-        rows = pl.ds(row + 16 * half, 16)
-        lhs[rows, lane : lane + LANES] = high
-        lhs[rows, 2 * LANES + lane : 3 * LANES + lane] = low
+def store_split(lhs, row, values):
+    for i, (first, second) in enumerate(values):
+        both = jnp.concatenate([first, second], axis=1)
+        high = both.astype(BF16)
+        low = (both - high.astype(F32)).astype(BF16)
+        rows = slice(row + 8 * i, row + 8 * i + 8)
+        lhs[rows, : 2 * LANES] = high
+        lhs[rows, 2 * LANES :] = low
 
 
 def product(lhs, weight):
@@ -197,7 +192,7 @@
 
 def spectral_pass(field, table, twiddle, weight, left, result, batch, side=None):
     groups = batch // 8
-    width = 64 // batch
+    width = 2
     steps = 8 // width
 
     def row_of(values, part, p, q):
@@ -224,8 +219,7 @@
                 c_mul(x[q], (row_of(twiddle, 0, p, q), row_of(twiddle, 1, p, q)))
                 for q in range(8)
             ]
-            store_split(lhs, row, [v[0] for v in x], 0)
-            store_split(lhs, row, [v[1] for v in x], LANES)
+            store_split(lhs, row, x)
 
     def transfer(step, values, lhs):
         for p, rows, row in places(step):
@@ -234,8 +228,7 @@
                 at = result_rows(row, q)
                 value = (values[at, :LANES], values[at, LANES:])
                 x.append(c_mul(value, (table_row(0, p, q), table_row(1, p, q))))
-            store_split(lhs, row, [v[1] for v in x], 0)
-            store_split(lhs, row, [v[0] for v in x], LANES)
+            store_split(lhs, row, [(v[1], v[0]) for v in x])
 
     def inverse(step, values):
         for p, rows, row in places(step):
@@ -264,8 +257,7 @@
     multiply(inverse_left[0], inverse_result[0])
     forward(2, forward_left[0])
 
-    def two_steps(i, carry, more=True):
-        step = 2 * i
+    def two_steps(step):
         multiply(forward_left[0], forward_result[0])
         transfer(step - 1, forward_result[1], inverse_left[1])
         multiply(inverse_left[1], inverse_result[1])
@@ -275,13 +267,8 @@
         transfer(step, forward_result[0], inverse_left[0])
         multiply(inverse_left[0], inverse_result[0])
         inverse(step - 1, inverse_result[1])
-        if more:
-            forward(step + 2, forward_left[0])
-        return carry
-
-    if steps > 4:
-        lax.fori_loop(1, steps // 2 - 1, two_steps, 0)
-    two_steps(steps // 2 - 1, 0, more=False)
+
+    two_steps(2)
     transfer(steps - 1, forward_result[1], inverse_left[1])
     multiply(inverse_left[1], inverse_result[1])
     inverse(steps - 2, inverse_result[0])
@@ -306,13 +293,12 @@
 
 
 def swap_halves(even, odd, low):
-    first = jnp.where(low, even, pltpu.roll(odd, LANES // 2, 1))
-    second = jnp.where(low, pltpu.roll(even, LANES // 2, 1), odd)
-    return first, second
+    crossed = pltpu.roll(jnp.where(low, odd, even), LANES // 2, 1)
+    return jnp.where(low, even, crossed), jnp.where(low, crossed, odd)
 
 
 def eight_rows(g):
-    return pl.ds(g * 8 if isinstance(g, int) else pl.multiple_of(g * 8, 8), 8)
+    return pl.ds(pl.multiple_of(g * 8, 8), 8)
 
 
 def pack_screen(j, scales, screen, moved, device, low):
@@ -357,8 +343,8 @@
 
     low = low_half((8, LANES))
 
-    def first(g, carry):
-        rows = eight_rows(g)
+    def first(g):
+        rows = slice(8 * g, 8 * g + 8)
         for b in range(8):
             x = []
             for a in range(8):
@@ -366,9 +352,9 @@
                 lanes = slice(n1 * LANES, (n1 + 1) * LANES)
                 x.append((beam[0, rows, lanes], beam[1, rows, lanes]) if a < 4 else None)
             enter(field, b, rows, x)
-        return carry
-
-    lax.fori_loop(0, 4, first, 0)
+
+    for g in range(4):
+        first(g)
     for copy in (copies[2], *copies[4:]):
         copy.wait()
     low_packed = low_half((32, LANES))
@@ -476,7 +462,11 @@
                 for a in range(8):
                     n1 = 8 * a + b
                     even, odd = arrived[2 * n1, packed], arrived[2 * n1 + 1, packed]
-                    x[a] = c_mul(x[a], phasor(swap_halves(even, odd, low)[half]))
+                    if half == 0:
+                        turns = jnp.where(low, even, pltpu.roll(odd, LANES // 2, 1))
+                    else:
+                        turns = jnp.where(low, pltpu.roll(even, LANES // 2, 1), odd)
+                    x[a] = c_mul(x[a], phasor(turns))
                 enter(field, b, rows, x)
         return carry
 
@@ -504,21 +494,21 @@
 ):
     low = low_half((8, LANES))
 
-    def first(g, carry):
-        rows = eight_rows(g)
+    def first(g):
+        rows = slice(8 * g, 8 * g + 8)
         for b in range(8):
             x = []
             for a in range(8):
                 n1 = 8 * a + b
                 x.append(swap_halves(arrived[2 * n1, rows], arrived[2 * n1 + 1, rows], low))
             enter(field, b, rows, x)
-        return carry
-
-    lax.fori_loop(0, 4, first, 0)
+
+    for g in range(4):
+        first(g)
     spectral_pass(field, (tables, 1), twiddle, weight, (l0, l1, l2, l3), (r0, r1, r2, r3), 32)
 
-    def last(g, carry):
-        rows = eight_rows(g)
+    def last(g):
+        rows = slice(8 * g, 8 * g + 8)
         for b in range(8):
             x = leave(field, b, rows)
             for a in range(4):
@@ -528,15 +518,15 @@
                 output[0, rows, lanes] = value[0]
                 output[1, rows, lanes] = value[1]
         leaving(g).start()
-        return carry
 
     def leaving(g):
-        rows = eight_rows(g)
+        rows = slice(8 * g, 8 * g + 8)
         return pltpu.make_async_copy(
             output.at[:, rows], output_in_hbm.at[:, rows], departure.at[g]
         )
 
-    lax.fori_loop(0, 4, last, 0)
+    for g in range(4):
+        last(g)
     for g in range(4):
         leaving(g).wait()
 
@@ -545,8 +535,8 @@
     space = {"s": pltpu.SMEM, "v": pltpu.VMEM, "h": pltpu.HBM}
     scratch = [
         pltpu.VMEM((2, 8, 8, batch, LANES), F32),
-        *[pltpu.VMEM((512, 4 * LANES), BF16)] * 4,
-        *[pltpu.VMEM((512, 2 * LANES), F32)] * 4,
+        *[pltpu.VMEM((16 * batch, 4 * LANES), BF16)] * 4,
+        *[pltpu.VMEM((16 * batch, 2 * LANES), F32)] * 4,
     ] if batch else []
     return pl.pallas_call(
         kernel,

time: 138 us -> 133 us (0.964)
  Pallas kernels: 37.7 us -> 32.8 us
    pallas_call x1, Pallas kernels: 22.4 us -> 19.4 us  [body(): call(columns_kernel, 'hhhh', [(4096, LANES)], 64, extra, 4 * 10 ** 10, 'h...]
where the time goes in v4:
time: 133 us
  waiting for transfers between devices  49.6 us (37%)
  blocking collectives  38.1 us (29%)
  Pallas kernels  32.8 us (25%)
  starting transfers between devices  12 us (9%)
    all_to_all x1, waiting for transfers between devices, exchange(): return lax.all_to_all(blocks, AXES, split_axis=0, concat_axis=0, tiled=True)  49.6 us
    all_to_all x1, blocking collectives, exchange(): return lax.all_to_all(blocks, AXES, split_axis=0, concat_axis=0, tiled=True)  38.1 us
    pallas_call x1, Pallas kernels, body(): call(columns_kernel, 'hhhh', [(4096, LANES)], 64, extra, 4 * 10 ** 10, 'h...  19.4 us
    all_to_all x1, starting transfers between devices, exchange(): return lax.all_to_all(blocks, AXES, split_axis=0, concat_axis=0, tiled=True)  12 us
    pallas_call x1, Pallas kernels, body(): call(first_rows_kernel, 'hhhhhhh', [(128, 64, LANES)], 32, extra, 10 ** 1...  6.38 us
    pallas_call x1, Pallas kernels, body(): call(last_rows_kernel, 'vvvvv', [(2, 32, 4096)], 32, extra, 10 ** 10, 'h')  4.29 us
    pallas_call x1, Pallas kernels, body(): call(tables_kernel, 'sssvh', [(2, *table), (2, 32, 4096)], 0, [], 10 ** 9...  2.79 us
  transfers between devices with their start and end apart: 1, of which 1 were waited for; matrix products, arithmetic and copies ran while one was open for 0% of the time, Pallas kernels for 2%

profile of v4, /device:TPU:1, one launch (start us, length us, event | category | flops | bytes accessed | tf_op | source)
XLA Modules:
  0.0 132.8 jit_solution(13732055667565594904)
XLA Ops:
  0.0 6.4 %shard_map.91.moved = f32[128,64,128]{2,1,0:T(8,128)} custom-call(s32[2]{0:T(128)} %offsets.1, f32[2]{0:T(128)} %distances.1, f32[1,64,64]{2,1,0:T(8,128)} %scales_in.1, f32[2,32,4096]{2,1,0:T(8,128)} %beam_in.1, s32[1,64,8192]{2,1,0:T(8,128)} %screen_in.1, f32[2,8,8,128]{3,2,1,0:T(8,128)} %constant.4.clone.twiddle_in.twiddle, ...), custom_call_target="tpu_custom_call" | custom-call | flops 10000000000 | bytes 4194304 | tf_op jit(solution)/shard_map/pallas_call | solution.py:572
  6.4 12.0 %all-to-all-start = ((f32[128,64,128]{2,1,0:T(8,128)}), f32[128,64,128]{2,1,0:T(8,128)}, u32[]{:S(2)}, u32[]{:S(2)}) async-start(f32[128,64,128]{2,1,0:T(8,128)} %shard_map.91.moved), calls=%async_computation | async-start | bytes 8388608 | tf_op jit(solution)/shard_map/all_to_all | solution.py:553
  18.4 2.8 %shard_map.92 = (f32[2,2,8,8,128]{4,3,2,1,0:T(8,128)}, f32[2,32,4096]{2,1,0:T(8,128)}) custom-call(s32[2]{0:T(128)} %offsets.1, f32[2]{0:T(128)} %distances.1, f32[32,32]{1,0:T(8,128)} %scales.1, s32[32,4096]{1,0:T(8,128)} %screen.1, f32[128,64,128]{2,1,0:T(8,128)} %shard_map.91.moved), custom_call_target="tpu_custom_call" | custom-call | flops 1000000000 | bytes 4194304 | tf_op jit(solution)/shard_map/pallas_call | solution.py:575
  21.2 49.6 %all-to-all-done.arrived_in = f32[128,64,128]{2,1,0:T(8,128)} async-done(((f32[128,64,128]{2,1,0:T(8,128)}), f32[128,64,128]{2,1,0:T(8,128)}, u32[]{:S(2)}, u32[]{:S(2)}) %all-to-all-start) | async-done | bytes 4194336 | tf_op jit(solution)/shard_map/all_to_all | solution.py:553
  70.7 19.4 %shard_map.93 = f32[4096,128]{1,0:T(8,128)} custom-call(f32[128,64,128]{2,1,0:T(8,128)} %all-to-all-done.arrived_in, f32[2,2,8,8,128]{4,3,2,1,0:T(8,128)} %get-tuple-element.7.tables_in.tables, f32[2,8,8,128]{3,2,1,0:T(8,128)} %constant.4.clone.twiddle_in.twiddle, bf16[768,256]{1,0:T(8,128)(2,1)} %constant.5.clone.weight_in.weight), custom_call_target="tpu_custom_call" | custom-call | flops 40000000000 | bytes 4194304 | tf_op jit(solution)/shard_map/pallas_call | solution.py:588
  90.1 0.0 copy-start
  90.1 0.0 copy-start.1
  90.1 0.0 copy-start.2
  90.1 0.0 copy-start.3
  90.1 38.1 %all_to_all.10.arrived = f32[128,32,128]{2,1,0:T(8,128)S(1)} all-to-all(f32[128,32,128]{2,1,0:T(8,128)} %bitcast.1), channel_id=1, replica_groups=mesh['gx'=8,'gy'=16] {'gx','gy'}, dimensions={0} | all-to-all | bytes 4194304 | tf_op jit(solution)/shard_map/all_to_all | solution.py:553
  128.3 0.0 copy-done
  128.3 0.0 copy-done.1
  128.3 0.0 copy-done.2
  128.3 0.0 copy-done.3
  128.3 4.3 %shard_map.94 = f32[2,32,4096]{2,1,0:T(8,128)} custom-call(f32[128,32,128]{2,1,0:T(8,128)S(1)} %all_to_all.10.arrived, f32[2,2,8,8,128]{4,3,2,1,0:T(8,128)S(1)} %copy-done.1, f32[2,32,4096]{2,1,0:T(8,128)S(1)} %copy-done, f32[2,8,8,128]{3,2,1,0:T(8,128)S(1)} %copy-done.3, bf16[768,256]{1,0:T(8,128)(2,1)S(1)} %copy-done.2), custom_call_target="tpu_custom_call" | custom-call | flops 10000000000 | bytes 4194304 | tf_op jit(solution)/shard_map/pallas_call | solution.py:593
Async XLA Ops:
  6.4 64.3 %all-to-all-start = ((f32[128,64,128]{2,1,0:T(8,128)}), f32[128,64,128]{2,1,0:T(8,128)}, u32[]{:S(2)}, u32[]{:S(2)}) async-start(f32[128,64,128]{2,1,0:T(8,128)} %shard_map.91.moved), calls=%async_computation | async-start | bytes 8388608 | tf_op jit(solution)/shard_map/all_to_all | solution.py:553
  90.1 38.2 %copy-start = (f32[2,32,4096]{2,1,0:T(8,128)S(1)}, f32[2,32,4096]{2,1,0:T(8,128)}, u32[]{:S(2)}) copy-start(f32[2,32,4096]{2,1,0:T(8,128)} %get-tuple-element.8.phasors) | copy-start | bytes 3145732
  90.1 38.2 %copy-start.1 = (f32[2,2,8,8,128]{4,3,2,1,0:T(8,128)S(1)}, f32[2,2,8,8,128]{4,3,2,1,0:T(8,128)}, u32[]{:S(2)}) copy-start(f32[2,2,8,8,128]{4,3,2,1,0:T(8,128)} %get-tuple-element.7.tables_in.tables) | copy-start | bytes 393220
  90.1 38.2 %copy-start.2 = (bf16[768,256]{1,0:T(8,128)(2,1)S(1)}, bf16[768,256]{1,0:T(8,128)(2,1)}, u32[]{:S(2)}) copy-start(bf16[768,256]{1,0:T(8,128)(2,1)} %constant.5.clone.weight_in.weight) | copy-start | bytes 1179652
  90.1 38.2 %copy-start.3 = (f32[2,8,8,128]{3,2,1,0:T(8,128)S(1)}, f32[2,8,8,128]{3,2,1,0:T(8,128)}, u32[]{:S(2)}) copy-start(f32[2,8,8,128]{3,2,1,0:T(8,128)} %constant.4.clone.twiddle_in.twiddle) | copy-start | bytes 196612
